TPU v7x, 32 devices: a whole 2x2x4 slice. The times are simulated.
32 devices in a mesh: seq: 16 (over z, y, x), head: 2 (over core).
Axes of the slice: x: 2, y: 2, z: 4, core: 2. Of those that a mesh axis runs over, the one named last changes fastest.
Arguments:
- raw_keys: bfloat16 [2, 16384, 8, 128], P(None, 'seq', 'head'), may hold values from -6 to 6
- raw_values: bfloat16 [2, 16384, 8, 128], P(None, 'seq', 'head'), may hold values from -6 to 6
- phase: int32 [2], replicated, may hold values from 0 to 255, as said below
- ratio: int32 [2, 16], replicated, may hold values from 8 to 32, as said below
- resident_len: int32 [2, 16], replicated, may hold values from 1 to 256, as said below
- beacon_queries: bfloat16 [2, 2048, 8, 8, 128], P(None, 'seq', 'head'), may hold values from -150 to 150
- beacon_wk: bfloat16 [8192, 1024], P('seq', 'head'), may hold values from -0.125 to 0.125
- beacon_wv: bfloat16 [8192, 1024], P('seq', 'head'), may hold values from -0.125 to 0.125
- resident_keys: bfloat16 [2, 4096, 8, 128], P(None, 'seq', 'head'), may hold values from -6 to 6
- resident_values: bfloat16 [2, 4096, 8, 128], P(None, 'seq', 'head'), may hold values from -6 to 6
- decode_queries: bfloat16 [4, 2, 8, 8, 128], P(None, None, 'head'), may hold values from -150 to 150
- out_weight: bfloat16 [8192, 8192], P('head', 'seq'), may hold values from -0.0625 to 0.0625
Outputs:
- beacon_keys: bfloat16 [2, 2048, 8, 128], P(None, 'seq', 'head')
- beacon_values: bfloat16 [2, 2048, 8, 128], P(None, 'seq', 'head')
- projected: bfloat16 [4, 2, 8192], P(None, None, 'seq')
Inputs may be any that keep to these rules, and one draw needn't show every extreme that they name: `phase`: some request has 255. `ratio`: each value is 1024 // 128 times 1, 2 or 4; both ends occur. `resident_len`: some pair has 256.
All inputs are finite; a program needn't handle non-finite values.
Results may differ from a plain program's by a relative error of at most 0.025.
Values may be sent and summed in bfloat16 or wider, within the bound.
A program may use at most 64 MiB of HBM per device.

v0:
```python
import functools
import math

import jax
import jax.numpy as jnp
from jax import lax
from jax.experimental import pallas as pl
from jax.experimental.pallas import tpu as pltpu
from jax.sharding import PartitionSpec as P

G = 8
INTERVAL = 1024
NB = 128
OFF = 256
STEPS = 4


masked_score = -1e30


def shifted(value, axis, steps):
    count = lax.axis_size(axis)
    first, last = (max(0, -steps), min(count, count - steps))
    return lax.ppermute(value, axis, [(source, source + steps) for source in range(first, last)])


def joined(shard, axis, combine):
    everything = jax.tree.map(lambda part: lax.all_gather(part, axis), shard)
    first = jax.tree.map(lambda part: part[0], everything)

    def hop(k, so_far):
        return combine(so_far, jax.tree.map(lambda part: part[k], everything))

    return lax.fori_loop(1, lax.axis_size(axis), hop, first)


def blend(former, latter):
    row_peak = jnp.maximum(former[0], latter[0])
    former_scale = jnp.exp(former[0] - row_peak)
    latter_scale = jnp.exp(latter[0] - row_peak)
    weight_sum = former[1] * former_scale + latter[1] * latter_scale
    weighted = former[2] * former_scale[..., None] + latter[2] * latter_scale[..., None]
    return (row_peak, weight_sum, weighted)


def pool_part(queries, key_rows, value_rows, positions, present, reaches):
    inv_root = 1.0 / math.sqrt(queries.shape[-1])

    def per_request(members):
        query_block, key_block, value_block, position_row, present_row, reach_row = members
        scores = (
            jnp.einsum("jkgd,ikd->jkgi", query_block, key_block, preferred_element_type=jnp.float32)
            * inv_root
        )
        allowed = (
            present_row[None, :]
            & (position_row[None, :] >= 0)
            & (position_row[None, :] < INTERVAL)
            & (position_row[None, :] < reach_row[:, None])
        )
        cache_mask = allowed[:, None, None, :]
        row_peak = jnp.max(jnp.where(cache_mask, scores, masked_score), axis=-1)
        weights = jnp.where(cache_mask, jnp.exp(scores - row_peak[..., None]), 0.0)
        weight_sum = jnp.sum(weights, axis=-1)
        weighted = jnp.einsum(
            "jkgi,ikd->jkgd",
            weights.astype(jnp.bfloat16),
            value_block,
            preferred_element_type=jnp.float32,
        )
        return (row_peak, weight_sum, weighted)

    return lax.map(per_request, (queries, key_rows, value_rows, positions, present, reaches))


def body(
    raw_keys,
    raw_values,
    phase,
    ratio,
    resident_len,
    beacon_queries,
    beacon_wk,
    beacon_wv,
    resident_keys,
    resident_values,
    decode_queries,
    out_weight,
):
    requests = raw_keys.shape[0]
    kv_local = raw_keys.shape[2]
    head_dim = raw_keys.shape[3]
    shard_index = lax.axis_index("seq")
    shard_count = lax.axis_size("seq")
    is_first = shard_index == 0
    is_last = shard_index == shard_count - 1
    own_ratio = lax.dynamic_index_in_dim(ratio, shard_index, 1, keepdims=False)
    slot_ids = jnp.arange(NB, dtype=jnp.int32)
    lead_in = jnp.where(is_first, phase, 0)
    reaches = (slot_ids[None, :] + 1) * own_ratio[:, None] + lead_in[:, None]
    tail_keys = raw_keys[:, INTERVAL - OFF :]
    tail_values = raw_values[:, INTERVAL - OFF :]
    own_positions = jnp.arange(INTERVAL, dtype=jnp.int32)[None, :] + phase[:, None]
    rim_ids = jnp.arange(OFF, dtype=jnp.int32)
    rim_positions = rim_ids[None, :] - OFF + phase[:, None]
    near_keys, near_values = shifted((tail_keys, tail_values), "seq", 1)
    key_rows = jnp.concatenate([near_keys, raw_keys], axis=1)
    value_rows = jnp.concatenate([near_values, raw_values], axis=1)
    positions = jnp.concatenate([rim_positions, own_positions], axis=1)
    present = jnp.logical_not(is_first) | (positions >= phase[:, None])
    pooled_parts = pool_part(beacon_queries, key_rows, value_rows, positions, present, reaches)
    pooled = (pooled_parts[2] / pooled_parts[1][..., None]).astype(jnp.bfloat16)
    pooled_flat = pooled.reshape(requests * NB, kv_local * G * head_dim)
    pooled_whole = lax.all_gather(pooled_flat, "head", axis=1, tiled=True)
    key_sum = jnp.dot(
        pooled_whole,
        lax.all_gather(beacon_wk, "seq", axis=0, tiled=True),
        preferred_element_type=jnp.float32,
    )
    value_sum = jnp.dot(
        pooled_whole,
        lax.all_gather(beacon_wv, "seq", axis=0, tiled=True),
        preferred_element_type=jnp.float32,
    )
    made_keys = key_sum
    made_values = value_sum
    made_keys = made_keys.reshape(requests, NB, kv_local, head_dim)
    made_values = made_values.reshape(requests, NB, kv_local, head_dim)
    slot_live = slot_ids[None, :] < (INTERVAL // own_ratio)[:, None]
    beacon_keys = jnp.where(slot_live[:, :, None, None], made_keys, 0.0).astype(jnp.bfloat16)
    beacon_values = jnp.where(slot_live[:, :, None, None], made_values, 0.0).astype(jnp.bfloat16)
    cache_keys = jnp.concatenate([resident_keys, beacon_keys, tail_keys], axis=1)
    cache_values = jnp.concatenate([resident_values, beacon_values, tail_values], axis=1)
    own_len = lax.dynamic_index_in_dim(resident_len, shard_index, 1, keepdims=False)
    resident_ok = jnp.arange(resident_keys.shape[1], dtype=jnp.int32)[None, :] < own_len[:, None]
    leftover_ok = (rim_ids[None, :] >= OFF - phase[:, None]) & is_last
    usable = jnp.concatenate([resident_ok, slot_live, leftover_ok], axis=1)
    inv_root = 1.0 / math.sqrt(head_dim)
    scores = (
        jnp.einsum(
            "srkgd,rikd->rksgi", decode_queries, cache_keys, preferred_element_type=jnp.float32
        )
        * inv_root
    )
    cache_mask = usable[:, None, None, None, :]
    row_peak = jnp.max(jnp.where(cache_mask, scores, masked_score), axis=-1)
    weights = jnp.where(cache_mask, jnp.exp(scores - row_peak[..., None]), 0.0)
    weight_sum = jnp.sum(weights, axis=-1)
    weighted = jnp.einsum(
        "rksgi,rikd->rksgd",
        weights.astype(jnp.bfloat16),
        cache_values,
        preferred_element_type=jnp.float32,
    )
    merged = joined((row_peak, weight_sum, weighted), "seq", blend)
    total_sum = merged[1]
    total_weighted = merged[2]
    attended = (total_weighted / total_sum[..., None]).astype(jnp.bfloat16)
    attended = jnp.transpose(attended, (2, 0, 1, 3, 4)).reshape(
        STEPS * requests, kv_local * G * head_dim
    )
    partial_value = jnp.dot(attended, out_weight, preferred_element_type=jnp.float32)
    summed = lax.psum(partial_value, "head")
    projected = summed.astype(jnp.bfloat16).reshape(STEPS, requests, out_weight.shape[1])
    return (beacon_keys, beacon_values, projected)


B = 4
CH = 4


def fused_kernel(
    shard_count,
    phase_ref,
    ratio_ref,
    rlen_ref,
    k_hbm,
    v_hbm,
    q_hbm,
    wk_hbm,
    wv_hbm,
    rk_raw,
    rv_raw,
    dq_ref,
    ow_hbm,
    bk_ref,
    bv_ref,
    proj_ref,
    kbuf,
    vbuf,
    qbuf,
    wbuf,
    act,
    stage,
    psend,
    precv,
    own,
    bias,
    owbuf,
    rk_ref,
    rv_ref,
    snd,
    snd_stats,
    rcv,
    rcv_stats,
    att,
    part,
    load_sem,
    rim_send,
    rim_recv,
    w_send,
    w_recv,
    a_send,
    a_recv,
    a_loc,
    p_send,
    p_recv,
    s_send,
    s_recv,
    d_send,
    d_recv,
    e_send,
    e_recv,
    t_send,
    t_recv,
    h_send,
    h_recv,
):
    n = shard_count
    depth = n // B
    s = lax.axis_index("seq")
    h = lax.axis_index("head")
    z = s // B
    me = lax.rem(s, B)
    heads, rows, hd = kbuf.shape[1], kbuf.shape[2], kbuf.shape[3]
    requests = kbuf.shape[0]
    interval = rows - OFF
    nb = bias.shape[1]
    width = wbuf.shape[3]
    inv_root = 1.0 / math.sqrt(hd)
    f32 = jnp.float32

    def remote(src, dst, send, recv, seq=None):
        target = {"head": 1 - h} if seq is None else {"seq": seq}
        return pltpu.make_async_remote_copy(
            src_ref=src,
            dst_ref=dst,
            send_sem=send,
            recv_sem=recv,
            device_id=target,
            device_id_type=pl.DeviceIdType.MESH,
        )

    loads = []
    half = wk_hbm.shape[1] // (CH // 2)
    for c in range(CH):
        source = (wk_hbm, wv_hbm)[c // (CH // 2)]
        first = (c % (CH // 2)) * half
        loads.append(
            pltpu.make_async_copy(
                source.at[:, first : first + half], wbuf.at[z, c], load_sem.at[c]
            )
        )
    loads.append(pltpu.make_async_copy(k_hbm, kbuf.at[:, :, OFF:], load_sem.at[CH]))
    loads.append(pltpu.make_async_copy(v_hbm, vbuf.at[:, :, OFF:], load_sem.at[CH + 1]))
    loads.append(pltpu.make_async_copy(q_hbm, qbuf, load_sem.at[CH + 2]))
    loads.append(pltpu.make_async_copy(ow_hbm, owbuf, load_sem.at[CH + 3]))
    for copy in loads:
        copy.start()

    barrier = pltpu.get_barrier_semaphore()
    for o in range(1, n):
        pl.semaphore_signal(
            barrier, inc=1, device_id={"seq": lax.rem(s + o, n)}, device_id_type=pl.DeviceIdType.MESH
        )
    pl.semaphore_signal(
        barrier, inc=1, device_id={"head": 1 - h}, device_id_type=pl.DeviceIdType.MESH
    )
    pl.semaphore_wait(barrier, n)

    def rim(which, k):
        source, target = ((k_hbm, kbuf), (v_hbm, vbuf))[which]
        return remote(
            source.at[:, k, interval - OFF :],
            target.at[:, k, :OFF],
            rim_send.at[which, k],
            rim_recv.at[which, k],
            lax.rem(s + 1, n),
        )

    @pl.when(s < n - 1)
    def _():
        for k in range(heads):
            rim(0, k).start()
            rim(1, k).start()

    @pl.when(s == 0)
    def _():
        kbuf[:, :, :OFF] = jnp.zeros((requests, heads, OFF, hd), kbuf.dtype)
        vbuf[:, :, :OFF] = jnp.zeros((requests, heads, OFF, hd), vbuf.dtype)

    def w_copy(way, d, c, shard, target):
        return remote(
            wbuf.at[shard, c],
            wbuf.at[shard, c],
            w_send.at[way, d, c],
            w_recv.at[way, d, c],
            target * B + me,
        )

    def w_out(way, d):
        if way == 0:
            return z - d, z + 1, (z - d >= 0) & (z + 1 < depth)
        return z + d, z - 1, (z + d < depth) & (z - 1 >= 0)

    def w_in(way, d):
        if way == 0:
            return z - 1 - d, z - 1 - d >= 0
        return z + 1 + d, z + 1 + d < depth

    def w_start(d, c):
        for way in range(2):
            shard, target, there = w_out(way, d)

            @pl.when(there)
            def _(way=way, shard=shard, target=target):
                w_copy(way, d, c, shard, target).start()

    def w_wait(d, c):
        for way in range(2):
            shard, there = w_in(way, d)

            @pl.when(there)
            def _(way=way, shard=shard):
                w_copy(way, d, c, shard, z).wait_recv()

    def w_relay(d, c):
        for way in range(2):
            shard, there = w_in(way, d - 1)
            out, target, onward = w_out(way, d)

            @pl.when(there)
            def _(way=way, shard=shard):
                w_copy(way, d - 1, c, shard, z).wait_recv()

            @pl.when(onward)
            def _(way=way, out=out, target=target):
                w_copy(way, d, c, out, target).start()

    def w_own(c):
        loads[c].wait()
        w_start(0, c)

    for c in range(CH):
        w_own(c)

    for r in range(requests):
        slot = lax.broadcasted_iota(jnp.int32, (nb, rows), 0)
        position = lax.broadcasted_iota(jnp.int32, (nb, rows), 1) - OFF + phase_ref[r]
        lead = jnp.where(s == 0, phase_ref[r], 0)
        reach = (slot + 1) * ratio_ref[r, s] + lead
        allowed = (position >= lead) & (position < interval) & (position < reach)
        bias[r] = jnp.where(allowed, 0.0, masked_score).astype(f32)

    loads[CH].wait()
    loads[CH + 1].wait()
    loads[CH + 2].wait()

    def a_remote(u, x):
        kk, r, y = u // 4, lax.rem(u, 2), lax.rem(u // 2, 2)
        return remote(
            stage.at[u, x],
            act.at[h * 2 + kk, me, r],
            a_send.at[u, x],
            a_recv.at[kk, r, me],
            z * B + y * 2 + x,
        )

    def a_local(kk, r, u):
        return pltpu.make_async_copy(
            stage.at[u, lax.rem(me, 2)], act.at[h * 2 + kk, me, r], a_loc.at[kk, r]
        )

    def a_relay(kk):
        return remote(
            act.at[h * 2 + kk], act.at[h * 2 + kk], p_send.at[kk], p_recv.at[kk]
        )

    def a_gather(kk):
        for r in range(requests):
            a_local(kk, r, kk * 4 + (me // 2) * 2 + r).wait()
            for o in range(1, B):
                source = lax.rem(me + o, B)
                remote(
                    stage.at[0, 0],
                    act.at[h * 2 + kk, source, r],
                    a_send.at[0, 0],
                    a_recv.at[kk, r, source],
                    s,
                ).wait_recv()
        a_relay(kk).start()

    def unit(u, carry):
        k, r = u // 2, lax.rem(u, 2)

        @pl.when((r == 0) & (s > 0))
        def _():
            rim(0, k).wait_recv()
            rim(1, k).wait_recv()

        for g in range(G):
            scores = (
                lax.dot_general(
                    qbuf[r, k, g],
                    kbuf[r, k],
                    (((1,), (1,)), ((), ())),
                    preferred_element_type=f32,
                )
                * inv_root
                + bias[r]
            )
            weights = jnp.exp(scores - jnp.max(scores, axis=-1, keepdims=True))
            total = jnp.sum(weights, axis=-1, keepdims=True)
            out = jnp.dot(weights.astype(jnp.bfloat16), vbuf[r, k], preferred_element_type=f32)
            at = (g % 4) * hd
            stage[u, g // 4, :, at : at + hd] = (out / total).astype(jnp.bfloat16)
        for x in range(2):
            member = lax.rem(k, 2) * 2 + x

            @pl.when(member == me)
            def _():
                a_local(u // 4, r, u).start()

            @pl.when(member != me)
            def _(x=x):
                a_remote(u, x).start()

        @pl.when(u == 3)
        def _():
            w_relay(1, 0)

        @pl.when(u == 6)
        def _():
            a_gather(0)

        return carry

    lax.fori_loop(0, 2 * heads, unit, 0)
    w_relay(2, 0)
    w_relay(1, 1)
    for r in range(requests):
        rk_ref[r] = jnp.swapaxes(rk_raw[r], 0, 1)
        rv_ref[r] = jnp.swapaxes(rv_raw[r], 0, 1)
    a_gather(1)
    w_relay(2, 1)
    w_relay(1, 2)
    a_relay(0).wait_recv()
    a_relay(1).wait_recv()

    def p_copy(c, to, frm):
        return remote(
            psend.at[to, c], precv.at[frm, c], s_send.at[to, c], s_recv.at[frm, c], z * B + to
        )

    slot_row = lax.broadcasted_iota(jnp.int32, (nb, width), 0)

    def finish(c):
        for o in range(1, B):
            source = lax.rem(me + o, B)
            p_copy(c, source, source).wait_recv()
        total = own[c]
        for o in range(1, B):
            total += precv[lax.rem(me + o, B), c].astype(f32)
        out_ref = (bk_ref, bv_ref)[c // (CH // 2)]
        at = (c % (CH // 2)) * width
        for r in range(requests):
            live = (slot_row + 1) * ratio_ref[r, s] <= interval
            out_ref[r * nb : (r + 1) * nb, at : at + width] = jnp.where(
                live, total[r * nb : (r + 1) * nb], 0.0
            ).astype(jnp.bfloat16)

    for c in range(CH):
        if c == 1:
            w_relay(2, 2)
            w_relay(1, 3)
        if c == 2:
            w_relay(2, 3)
        w_wait(depth - 2, c)

        def product(o, carry, c=c):
            to = lax.rem(me + 1 + o, B)
            total = jnp.zeros((requests * nb, width), f32)
            for zi in range(depth):
                total += jnp.dot(
                    act[zi, to].reshape(requests * nb, act.shape[4]),
                    wbuf[zi, c],
                    preferred_element_type=f32,
                )

            @pl.when(o < B - 1)
            def _():
                psend[to, c] = total.astype(jnp.bfloat16)
                p_copy(c, to, me).start()

            @pl.when(o == B - 1)
            def _():
                own[c] = total

            return carry

        lax.fori_loop(0, B, product, 0)
        if c > 0:
            finish(c - 1)
    finish(CH - 1)

    res = rk_ref.shape[2]
    qrows = dq_ref.shape[1]
    pair = qrows // G
    cells = res + nb + OFF
    row_request = lax.rem(lax.broadcasted_iota(jnp.int32, (qrows, cells), 0), pair) // (
        pair // requests
    )
    cell = lax.broadcasted_iota(jnp.int32, (qrows, cells), 1)
    last = jnp.where(s == n - 1, 1, 0)
    masks = []
    for r in range(requests):
        usable = (
            (cell < rlen_ref[r, s])
            | ((cell >= res) & (cell < res + nb) & ((cell - res + 1) * ratio_ref[r, s] <= interval))
            | ((cell >= res + nb + OFF - phase_ref[r] * last) & (cell >= res + nb))
        )
        masks.append(usable & (row_request == r))
    share = G * heads // n
    for k in range(heads):
        lanes = slice(k * hd, (k + 1) * hd)
        pieces = []
        for r in range(requests):
            keys = (rk_ref[r, k], bk_ref[r * nb : (r + 1) * nb, lanes], kbuf[r, k, rows - OFF :])
            scores = jnp.concatenate(
                [
                    lax.dot_general(
                        dq_ref[k], key, (((1,), (1,)), ((), ())), preferred_element_type=f32
                    )
                    for key in keys
                ],
                axis=1,
            )
            pieces.append(jnp.where(masks[r], scores * inv_root, masked_score))
        peak = jnp.maximum(
            jnp.max(pieces[0], axis=-1, keepdims=True), jnp.max(pieces[1], axis=-1, keepdims=True)
        )
        total = jnp.zeros((qrows, 1), f32)
        out = jnp.zeros((qrows, hd), f32)
        for r in range(requests):
            weights = jnp.exp(pieces[r] - peak)
            total += jnp.sum(weights, axis=-1, keepdims=True)
            low = weights.astype(jnp.bfloat16)
            out += jnp.dot(low[:, :res], rv_ref[r, k], preferred_element_type=f32)
            out += jnp.dot(
                low[:, res : res + nb],
                bv_ref[r * nb : (r + 1) * nb, lanes],
                preferred_element_type=f32,
            )
            out += jnp.dot(
                low[:, res + nb :], vbuf[r, k, rows - OFF :], preferred_element_type=f32
            )
        lane = lax.broadcasted_iota(jnp.int32, (qrows, hd), 1)
        slots = hd // (2 * share)
        stats = jnp.where(lax.rem(lane // slots, 2) == 0, peak, total)
        stats = stats.reshape(G // share, share, pair, hd)
        lane = lax.broadcasted_iota(jnp.int32, (G // share, pair, hd), 2)
        packed = stats[:, 0]
        for j in range(1, share):
            packed = jnp.where(lane >= 2 * slots * j, stats[:, j], packed)
        dests = slice(k * G // share, (k + 1) * G // share)
        snd[dests] = out.reshape(G // share, share * pair, hd).astype(jnp.bfloat16)
        snd_stats[dests] = packed

    def d_copy(to, frm):
        return remote(snd.at[to], rcv.at[frm], d_send.at[to], d_recv.at[frm], to)

    def e_copy(to, frm):
        return remote(snd_stats.at[to], rcv_stats.at[frm], e_send.at[to], e_recv.at[frm], to)

    def t_copy(to, frm):
        return remote(att.at[frm], att.at[frm], t_send.at[to], t_recv.at[frm], to)

    for o in range(1, n):
        e_copy(lax.rem(s + o, n), s).start()
        d_copy(lax.rem(s + o, n), s).start()
    rcv[s] = snd[s]
    rcv_stats[s] = snd_stats[s]
    for o in range(1, n):
        source = lax.rem(s + o, n)
        e_copy(source, source).wait_recv()
        d_copy(source, source).wait_recv()
    landed = rcv[...].astype(f32)
    attended = []
    for j in range(share):
        at = 2 * slots * j
        peaks = rcv_stats[:, :, at : at + 1]
        sums = rcv_stats[:, :, at + slots : at + slots + 1]
        scale = jnp.exp(peaks - jnp.max(peaks, axis=0, keepdims=True))
        mixed = jnp.sum(scale * landed[:, j * pair : (j + 1) * pair], axis=0)
        attended.append(mixed / jnp.sum(scale * sums, axis=0))
    att[s] = jnp.concatenate(attended, axis=0).astype(jnp.bfloat16)
    for o in range(1, n):
        t_copy(lax.rem(s + o, n), s).start()
    for o in range(1, n):
        source = lax.rem(s + o, n)
        t_copy(source, source).wait_recv()
    loads[CH + 3].wait()
    wide = [att[i].astype(f32) for i in range(n)]
    vectors = jnp.concatenate(
        [wide[i][j * pair : (j + 1) * pair] for i in range(n) for j in range(share)], axis=1
    ).astype(jnp.bfloat16)
    partial_value = jnp.dot(vectors, owbuf[...], preferred_element_type=f32)
    part[0] = partial_value
    swap = remote(part.at[0], part.at[1], h_send, h_recv)
    swap.start()
    swap.wait_recv()
    first = jnp.where(h == 0, part[0], part[1])
    second = jnp.where(h == 0, part[1], part[0])
    proj_ref[...] = (first + second).astype(jnp.bfloat16)

    swap.wait_send()
    for o in range(1, n):
        d_copy(lax.rem(s + o, n), s).wait_send()
        e_copy(lax.rem(s + o, n), s).wait_send()
        t_copy(lax.rem(s + o, n), s).wait_send()
    for c in range(CH):
        for o in range(1, B):
            p_copy(c, lax.rem(me + o, B), me).wait_send()
    a_relay(0).wait_send()
    a_relay(1).wait_send()
    for u in range(2 * heads):
        for x in range(2):

            @pl.when((u // 2 % 2) * 2 + x != me)
            def _(u=u, x=x):
                a_remote(jnp.int32(u), x).wait_send()

    for way in range(2):
        for d in range(depth - 1):
            shard, target, there = w_out(way, d)
            for c in range(CH):

                @pl.when(there)
                def _(way=way, d=d, c=c, shard=shard, target=target):
                    w_copy(way, d, c, shard, target).wait_send()

    @pl.when(s < n - 1)
    def _():
        for k in range(heads):
            rim(0, k).wait_send()
            rim(1, k).wait_send()


def fused_body(
    shard_count,
    raw_keys,
    raw_values,
    phase,
    ratio,
    resident_len,
    beacon_queries,
    beacon_wk,
    beacon_wv,
    resident_keys,
    resident_values,
    decode_queries,
    out_weight,
):
    n = shard_count
    depth = n // B
    requests, interval, heads, hd = raw_keys.shape
    steps = decode_queries.shape[0]
    nb = beacon_queries.shape[1]
    rows = interval + OFF
    by_head = (0, 2, 1, 3)
    feature, columns = beacon_wk.shape
    width = 2 * columns // CH
    pair = requests * steps
    share = G * heads // n
    bf16, f32 = jnp.bfloat16, jnp.float32
    dma = pltpu.SemaphoreType.DMA
    smem = pl.BlockSpec(memory_space=pltpu.SMEM)
    anywhere = pl.BlockSpec(memory_space=pl.ANY)
    vmem = pl.BlockSpec(memory_space=pltpu.VMEM)
    keys, values, projected = pl.pallas_call(
        functools.partial(fused_kernel, n),
        out_shape=(
            jax.ShapeDtypeStruct((requests * nb, columns), bf16),
            jax.ShapeDtypeStruct((requests * nb, columns), bf16),
            jax.ShapeDtypeStruct((pair, out_weight.shape[1]), bf16),
        ),
        in_specs=[smem] * 3 + [anywhere] * 5 + [vmem] * 3 + [anywhere],
        out_specs=(vmem, vmem, vmem),
        scratch_shapes=[
            pltpu.VMEM((requests, heads, rows, hd), bf16),
            pltpu.VMEM((requests, heads, rows, hd), bf16),
            pltpu.VMEM((requests, heads, G, nb, hd), bf16),
            pltpu.VMEM((depth, CH, feature, width), bf16),
            pltpu.VMEM((depth, B, requests, nb, feature), bf16),
            pltpu.VMEM((requests * heads, 2, nb, feature), bf16),
            pltpu.VMEM((B, CH, requests * nb, width), bf16),
            pltpu.VMEM((B, CH, requests * nb, width), bf16),
            pltpu.VMEM((CH, requests * nb, width), f32),
            pltpu.VMEM((requests, nb, rows), f32),
            pltpu.VMEM(out_weight.shape, bf16),
            pltpu.VMEM((requests, heads, resident_keys.shape[1], hd), bf16),
            pltpu.VMEM((requests, heads, resident_keys.shape[1], hd), bf16),
            pltpu.VMEM((n, share * pair, hd), bf16),
            pltpu.VMEM((n, pair, hd), f32),
            pltpu.VMEM((n, share * pair, hd), bf16),
            pltpu.VMEM((n, pair, hd), f32),
            pltpu.VMEM((n, share * pair, hd), bf16),
            pltpu.VMEM((2, pair, out_weight.shape[1]), f32),
            dma((CH + 4,)),
            dma((2, heads)),
            dma((2, heads)),
            dma((2, depth - 1, CH)),
            dma((2, depth - 1, CH)),
            dma((requests * heads, 2)),
            dma((2, requests, B)),
            dma((2, requests)),
            dma((2,)),
            dma((2,)),
            dma((B, CH)),
            dma((B, CH)),
            dma((n,)),
            dma((n,)),
            dma((n,)),
            dma((n,)),
            dma((n,)),
            dma((n,)),
            dma,
            dma,
        ],
        compiler_params=pltpu.CompilerParams(
            collective_id=0, has_side_effects=True, vmem_limit_bytes=60 * 1024 * 1024
        ),
    )(
        phase,
        ratio,
        resident_len,
        jnp.transpose(raw_keys, by_head),
        jnp.transpose(raw_values, by_head),
        jnp.transpose(beacon_queries, (0, 2, 3, 1, 4)),
        beacon_wk,
        beacon_wv,
        resident_keys,
        resident_values,
        jnp.transpose(decode_queries, (2, 3, 1, 0, 4)).reshape(heads, G * pair, hd),
        out_weight,
    )
    return (
        keys.reshape(requests, nb, heads, hd),
        values.reshape(requests, nb, heads, hd),
        jnp.transpose(projected.reshape(requests, steps, -1), (1, 0, 2)),
    )


def chosen_body(shard_count, head_count):
    def run(*arrays):
        requests, _, heads, hd = arrays[0].shape
        feature = arrays[6].shape[0]
        fits = (
            head_count == 2
            and shard_count == B * B
            and requests == 2
            and heads == B
            and 2 * feature == G * hd
        )
        return fused_body(shard_count, *arrays) if fits else body(*arrays)

    return run


def solution(mesh):
    return jax.shard_map(
        chosen_body(mesh.shape["seq"], mesh.shape["head"]),
        mesh=mesh,
        in_specs=(
            P(None, "seq", "head", None),
            P(None, "seq", "head", None),
            P(),
            P(),
            P(),
            P(None, "seq", "head", None, None),
            P("seq", "head"),
            P("seq", "head"),
            P(None, "seq", "head", None),
            P(None, "seq", "head", None),
            P(None, None, "head", None, None),
            P("head", "seq"),
        ),
        out_specs=(
            P(None, "seq", "head", None),
            P(None, "seq", "head", None),
            P(None, None, "seq"),
        ),
        check_vma=False,
    )
```

profile of v0, /device:TPU:0, one launch (start us, length us, event | category | flops | bytes accessed | tf_op | source)
XLA Modules:
  0.0 136.8 jit_solution(17787697863340303887)
XLA Ops:
  0.6 1.5 %copy.18 = bf16[4,8,2,4,128]{4,3,2,1,0:T(4,128)(2,1)} copy(bf16[4,8,2,4,128]{4,1,0,2,3:T(8,128)(2,1)} %bitcast.14) | data formatting | bytes 131072 | tf_op jit(solution)/shard_map/transpose | solution.py:754
  2.2 0.0 copy-start
  2.2 0.0 copy-start.1
  2.2 3.9 %copy.24 = bf16[2,128,4,8,128]{4,1,3,2,0:T(8,128)(2,1)} copy(bf16[2,128,4,8,128]{4,3,2,1,0:T(8,128)(2,1)} %param.17) | data formatting | bytes 4194304 | tf_op args[5]
  6.0 0.0 copy-done
  6.0 0.0 copy-done.1
  6.0 2.7 %copy_bitcast_fusion.1 = (bf16[2,4,1024,128]{3,2,1,0:T(8,128)(2,1)}, bf16[2,4,1024,128]{3,2,1,0:T(8,128)(2,1)}) fusion(bf16[2,1024,4,128]{3,2,1,0:T(4,128)(2,1)S(1)} %copy-done, bf16[2,1024,4,128]{3,2,1,0:T(4,128)(2,1)S(1)} %copy-done.1), kind=kLoop, calls=%fused_computation.1 | loop fusion | bytes 8388608 | tf_op jit(solution)/shard_map/transpose | solution.py:748
  8.7 123.3 %shard_map.139 = (bf16[256,512]{1,0:T(8,128)(2,1)}, bf16[256,512]{1,0:T(8,128)(2,1)}, bf16[8,512]{1,0:T(8,128)(2,1)}) custom-call(s32[2]{0:T(128)} %phase_ref.1, s32[2,16]{1,0:T(2,128)} %ratio_ref.1, s32[2,16]{1,0:T(2,128)} %rlen_ref.1, bf16[2,4,1024,128]{3,2,1,0:T(8,128)(2,1)} %get-tuple-element.10.k_hbm, bf16[2,4,1024,128]{3,2,1,0:T(8,128)(2,1)} %get-tuple-element.9.v_hbm, ...), custom_call_target="tpu_custom_call" | custom-call | tf_op jit(solution)/shard_map/pallas_call | solution.py:690
  132.0 1.7 %reshape.19 = bf16[2,128,4,128]{3,2,1,0:T(4,128)(2,1)} reshape(bf16[256,512]{1,0:T(8,128)(2,1)} %get-tuple-element.6) | data formatting | bytes 524288 | tf_op jit(solution)/shard_map/reshape | solution.py:758
  133.7 0.7 reshape.21
  134.4 0.6 copy.25
  135.1 1.7 %reshape.20 = bf16[2,128,4,128]{3,2,1,0:T(4,128)(2,1)} reshape(bf16[256,512]{1,0:T(8,128)(2,1)} %get-tuple-element.7) | data formatting | bytes 524288 | tf_op jit(solution)/shard_map/reshape | solution.py:759
Async XLA Ops:
  2.2 3.9 %copy-start = (bf16[2,1024,4,128]{3,2,1,0:T(4,128)(2,1)S(1)}, bf16[2,1024,4,128]{3,2,1,0:T(4,128)(2,1)}, u32[]{:S(2)}) copy-start(bf16[2,1024,4,128]{3,2,1,0:T(4,128)(2,1)} %param.13) | copy-start | bytes 6291460
  2.2 3.9 %copy-start.1 = (bf16[2,1024,4,128]{3,2,1,0:T(4,128)(2,1)S(1)}, bf16[2,1024,4,128]{3,2,1,0:T(4,128)(2,1)}, u32[]{:S(2)}) copy-start(bf16[2,1024,4,128]{3,2,1,0:T(4,128)(2,1)} %param.12) | copy-start | bytes 6291460
where the time goes:
time: 137 us
  Pallas kernels  123 us (90%)
  local copies, waits for them, and re-layouts  12.8 us (9%)
    pallas_call x1, Pallas kernels, fused_body(): pl.pallas_call(functools.partial(fused_kernel, n), out_shape=(jax.ShapeDt...  123 us
    unnamed x5, local copies, waits for them, and re-layouts  3.88 us

commit v1 on v0

v1 whole, which is shorter than its diff:
```python
import contextlib
import functools
import math

import jax
import jax.numpy as jnp
from jax import lax
from jax.experimental import pallas as pl
from jax.experimental.pallas import tpu as pltpu
from jax.sharding import PartitionSpec as P

G = 8
INTERVAL = 1024
NB = 128
OFF = 256
STEPS = 4


masked_score = -1e30


def region(name):
    return contextlib.nullcontext()


def shifted(value, axis, steps):
    count = lax.axis_size(axis)
    first, last = (max(0, -steps), min(count, count - steps))
    return lax.ppermute(value, axis, [(source, source + steps) for source in range(first, last)])


def joined(shard, axis, combine):
    everything = jax.tree.map(lambda part: lax.all_gather(part, axis), shard)
    first = jax.tree.map(lambda part: part[0], everything)

    def hop(k, so_far):
        return combine(so_far, jax.tree.map(lambda part: part[k], everything))

    return lax.fori_loop(1, lax.axis_size(axis), hop, first)


def blend(former, latter):
    row_peak = jnp.maximum(former[0], latter[0])
    former_scale = jnp.exp(former[0] - row_peak)
    latter_scale = jnp.exp(latter[0] - row_peak)
    weight_sum = former[1] * former_scale + latter[1] * latter_scale
    weighted = former[2] * former_scale[..., None] + latter[2] * latter_scale[..., None]
    return (row_peak, weight_sum, weighted)


def pool_part(queries, key_rows, value_rows, positions, present, reaches):
    inv_root = 1.0 / math.sqrt(queries.shape[-1])

    def per_request(members):
        query_block, key_block, value_block, position_row, present_row, reach_row = members
        scores = (
            jnp.einsum("jkgd,ikd->jkgi", query_block, key_block, preferred_element_type=jnp.float32)
            * inv_root
        )
        allowed = (
            present_row[None, :]
            & (position_row[None, :] >= 0)
            & (position_row[None, :] < INTERVAL)
            & (position_row[None, :] < reach_row[:, None])
        )
        cache_mask = allowed[:, None, None, :]
        row_peak = jnp.max(jnp.where(cache_mask, scores, masked_score), axis=-1)
        weights = jnp.where(cache_mask, jnp.exp(scores - row_peak[..., None]), 0.0)
        weight_sum = jnp.sum(weights, axis=-1)
        weighted = jnp.einsum(
            "jkgi,ikd->jkgd",
            weights.astype(jnp.bfloat16),
            value_block,
            preferred_element_type=jnp.float32,
        )
        return (row_peak, weight_sum, weighted)

    return lax.map(per_request, (queries, key_rows, value_rows, positions, present, reaches))


def body(
    raw_keys,
    raw_values,
    phase,
    ratio,
    resident_len,
    beacon_queries,
    beacon_wk,
    beacon_wv,
    resident_keys,
    resident_values,
    decode_queries,
    out_weight,
):
    requests = raw_keys.shape[0]
    kv_local = raw_keys.shape[2]
    head_dim = raw_keys.shape[3]
    shard_index = lax.axis_index("seq")
    shard_count = lax.axis_size("seq")
    is_first = shard_index == 0
    is_last = shard_index == shard_count - 1
    own_ratio = lax.dynamic_index_in_dim(ratio, shard_index, 1, keepdims=False)
    slot_ids = jnp.arange(NB, dtype=jnp.int32)
    lead_in = jnp.where(is_first, phase, 0)
    reaches = (slot_ids[None, :] + 1) * own_ratio[:, None] + lead_in[:, None]
    tail_keys = raw_keys[:, INTERVAL - OFF :]
    tail_values = raw_values[:, INTERVAL - OFF :]
    own_positions = jnp.arange(INTERVAL, dtype=jnp.int32)[None, :] + phase[:, None]
    rim_ids = jnp.arange(OFF, dtype=jnp.int32)
    rim_positions = rim_ids[None, :] - OFF + phase[:, None]
    near_keys, near_values = shifted((tail_keys, tail_values), "seq", 1)
    key_rows = jnp.concatenate([near_keys, raw_keys], axis=1)
    value_rows = jnp.concatenate([near_values, raw_values], axis=1)
    positions = jnp.concatenate([rim_positions, own_positions], axis=1)
    present = jnp.logical_not(is_first) | (positions >= phase[:, None])
    pooled_parts = pool_part(beacon_queries, key_rows, value_rows, positions, present, reaches)
    pooled = (pooled_parts[2] / pooled_parts[1][..., None]).astype(jnp.bfloat16)
    pooled_flat = pooled.reshape(requests * NB, kv_local * G * head_dim)
    pooled_whole = lax.all_gather(pooled_flat, "head", axis=1, tiled=True)
    key_sum = jnp.dot(
        pooled_whole,
        lax.all_gather(beacon_wk, "seq", axis=0, tiled=True),
        preferred_element_type=jnp.float32,
    )
    value_sum = jnp.dot(
        pooled_whole,
        lax.all_gather(beacon_wv, "seq", axis=0, tiled=True),
        preferred_element_type=jnp.float32,
    )
    made_keys = key_sum
    made_values = value_sum
    made_keys = made_keys.reshape(requests, NB, kv_local, head_dim)
    made_values = made_values.reshape(requests, NB, kv_local, head_dim)
    slot_live = slot_ids[None, :] < (INTERVAL // own_ratio)[:, None]
    beacon_keys = jnp.where(slot_live[:, :, None, None], made_keys, 0.0).astype(jnp.bfloat16)
    beacon_values = jnp.where(slot_live[:, :, None, None], made_values, 0.0).astype(jnp.bfloat16)
    cache_keys = jnp.concatenate([resident_keys, beacon_keys, tail_keys], axis=1)
    cache_values = jnp.concatenate([resident_values, beacon_values, tail_values], axis=1)
    own_len = lax.dynamic_index_in_dim(resident_len, shard_index, 1, keepdims=False)
    resident_ok = jnp.arange(resident_keys.shape[1], dtype=jnp.int32)[None, :] < own_len[:, None]
    leftover_ok = (rim_ids[None, :] >= OFF - phase[:, None]) & is_last
    usable = jnp.concatenate([resident_ok, slot_live, leftover_ok], axis=1)
    inv_root = 1.0 / math.sqrt(head_dim)
    scores = (
        jnp.einsum(
            "srkgd,rikd->rksgi", decode_queries, cache_keys, preferred_element_type=jnp.float32
        )
        * inv_root
    )
    cache_mask = usable[:, None, None, None, :]
    row_peak = jnp.max(jnp.where(cache_mask, scores, masked_score), axis=-1)
    weights = jnp.where(cache_mask, jnp.exp(scores - row_peak[..., None]), 0.0)
    weight_sum = jnp.sum(weights, axis=-1)
    weighted = jnp.einsum(
        "rksgi,rikd->rksgd",
        weights.astype(jnp.bfloat16),
        cache_values,
        preferred_element_type=jnp.float32,
    )
    merged = joined((row_peak, weight_sum, weighted), "seq", blend)
    total_sum = merged[1]
    total_weighted = merged[2]
    attended = (total_weighted / total_sum[..., None]).astype(jnp.bfloat16)
    attended = jnp.transpose(attended, (2, 0, 1, 3, 4)).reshape(
        STEPS * requests, kv_local * G * head_dim
    )
    partial_value = jnp.dot(attended, out_weight, preferred_element_type=jnp.float32)
    summed = lax.psum(partial_value, "head")
    projected = summed.astype(jnp.bfloat16).reshape(STEPS, requests, out_weight.shape[1])
    return (beacon_keys, beacon_values, projected)


B = 4
CH = 4


def fused_kernel(
    shard_count,
    phase_ref,
    ratio_ref,
    rlen_ref,
    k_hbm,
    v_hbm,
    q_hbm,
    wk_hbm,
    wv_hbm,
    rk_hbm,
    rv_hbm,
    dq_hbm,
    ow_hbm,
    bk_out,
    bv_out,
    proj_ref,
    kraw,
    vraw,
    qraw,
    rkraw,
    rvraw,
    dqraw,
    rimraw,
    rimrel,
    kbuf,
    vbuf,
    qbuf,
    wbuf,
    act,
    stage,
    psend,
    precv,
    own,
    bias,
    owbuf,
    rk_ref,
    rv_ref,
    dq_ref,
    bk_ref,
    bv_ref,
    snd,
    snd_stats,
    rcv,
    rcv_stats,
    att,
    part,
    load_sem,
    rim_send,
    rim_recv,
    rel_send,
    rel_recv,
    w_send,
    w_recv,
    a_send,
    a_recv,
    a_loc,
    p_send,
    p_recv,
    s_send,
    s_recv,
    d_send,
    d_recv,
    e_send,
    e_recv,
    t_send,
    t_recv,
    h_send,
    h_recv,
):
    n = shard_count
    depth = n // B
    s = lax.axis_index("seq")
    h = lax.axis_index("head")
    z = s // B
    me = lax.rem(s, B)
    requests, interval, heads, hd = kraw.shape
    rows = interval + OFF
    nb = bias.shape[1]
    width = wbuf.shape[3]
    inv_root = 1.0 / math.sqrt(hd)
    f32 = jnp.float32
    bf16 = jnp.bfloat16

    def remote(src, dst, send, recv, seq=None):
        target = {"head": 1 - h} if seq is None else {"seq": seq}
        return pltpu.make_async_remote_copy(
            src_ref=src,
            dst_ref=dst,
            send_sem=send,
            recv_sem=recv,
            device_id=target,
            device_id_type=pl.DeviceIdType.MESH,
        )

    loads = []

    def load(source, target):
        loads.append(pltpu.make_async_copy(source, target, load_sem.at[len(loads)]))
        loads[-1].start()
        return loads[-1]

    half = wk_hbm.shape[1] // (CH // 2)
    w_load = []
    for c in range(CH):
        source = (wk_hbm, wv_hbm)[c // (CH // 2)]
        first = (c % (CH // 2)) * half
        w_load.append(load(source.at[:, first : first + half], wbuf.at[z, c]))
    kv_load = [
        load((k_hbm, v_hbm)[p % 2].at[p // 2], (kraw, vraw)[p % 2].at[p // 2])
        for p in range(2 * requests)
    ]
    q_load = load(q_hbm, qraw)
    rest_load = [load(rk_hbm, rkraw), load(rv_hbm, rvraw), load(dq_hbm, dqraw)]
    ow_load = load(ow_hbm, owbuf)

    with region("barrier"):
        barrier = pltpu.get_barrier_semaphore()
        for o in range(1, n):
            pl.semaphore_signal(
                barrier,
                inc=1,
                device_id={"seq": lax.rem(s + o, n)},
                device_id_type=pl.DeviceIdType.MESH,
            )
        pl.semaphore_signal(
            barrier, inc=1, device_id={"head": 1 - h}, device_id_type=pl.DeviceIdType.MESH
        )
        pl.semaphore_wait(barrier, n)

    crosses = (me == B - 1) & (z < depth - 1)
    relays = (me < B - 1) & (z < depth - 1)

    def rim_near(p):
        source = (k_hbm, v_hbm)[p % 2].at[p // 2, interval - OFF :]
        return remote(source, rimraw.at[p], rim_send.at[p], rim_recv.at[p], lax.rem(s + 1, n))

    def rim_far(p):
        source = (k_hbm, v_hbm)[p % 2].at[p // 2, interval - OFF :]
        return remote(source, rimrel, rim_send.at[p], rel_recv, z * B + B - 1 - p)

    def rim_pass():
        p = B - 1 - me
        return remote(rimrel, rimraw.at[p], rel_send, rim_recv.at[p], lax.rem((z + 1) * B, n))

    @pl.when(me < B - 1)
    def _():
        for p in range(2 * requests):
            rim_near(p).start()

    @pl.when(crosses)
    def _():
        rim_near(0).start()
        for p in range(1, 2 * requests):
            rim_far(p).start()

    def w_copy(way, d, c, shard, target):
        return remote(
            wbuf.at[shard, c],
            wbuf.at[shard, c],
            w_send.at[way, d, c],
            w_recv.at[way, d, c],
            target * B + me,
        )

    def w_out(way, d):
        if way == 0:
            return z - d, z + 1, (z - d >= 0) & (z + 1 < depth)
        return z + d, z - 1, (z + d < depth) & (z - 1 >= 0)

    def w_in(way, d):
        if way == 0:
            return z - 1 - d, z - 1 - d >= 0
        return z + 1 + d, z + 1 + d < depth

    def w_own(c):
        w_load[c].wait()
        for way in range(2):
            shard, target, there = w_out(way, 0)

            @pl.when(there)
            def _(way=way, shard=shard, target=target):
                w_copy(way, 0, c, shard, target).start()

    def w_relay(d, c):
        for way in range(2):
            shard, target, onward = w_out(way, d)

            @pl.when(onward)
            def _(way=way, shard=shard, target=target):
                w_copy(way, d - 1, c, shard, z).wait_recv()
                w_copy(way, d, c, shard, target).start()

    def w_wait(c):
        for way in range(2):
            for d in range(depth - 1):
                shard, there = w_in(way, d)
                if d < depth - 2:
                    there = there & ((z == depth - 1) if way == 0 else (z == 0))

                @pl.when(there)
                def _(way=way, d=d, shard=shard):
                    w_copy(way, d, c, shard, z).wait_recv()

    with region("w_own"):
        for c in range(CH):
            w_own(c)

    with region("prep"):
        for r in range(requests):
            slot = lax.broadcasted_iota(jnp.int32, (nb, rows), 0)
            position = lax.broadcasted_iota(jnp.int32, (nb, rows), 1) - OFF + phase_ref[r]
            lead = jnp.where(s == 0, phase_ref[r], 0)
            reach = (slot + 1) * ratio_ref[r, s] + lead
            allowed = (position >= lead) & (position < interval) & (position < reach)
            bias[r] = jnp.where(allowed, 0.0, masked_score).astype(f32)
        for p in range(2 * requests):
            kv_load[p].wait()
            (kbuf, vbuf)[p % 2][p // 2, :, OFF:] = jnp.swapaxes((kraw, vraw)[p % 2][p // 2], 0, 1)
        for copy in rest_load:
            copy.wait()
        for r in range(requests):
            rk_ref[r] = jnp.swapaxes(rkraw[r], 0, 1)
            rv_ref[r] = jnp.swapaxes(rvraw[r], 0, 1)
        steps = dqraw.shape[0]
        pair = steps * requests
        for k in range(heads):
            asked = jnp.stack(
                [dqraw[t, r, k].astype(f32) for t in range(steps) for r in range(requests)], axis=0
            )
            dq_ref[k] = jnp.swapaxes(asked, 0, 1).reshape(G * pair, hd).astype(bf16)
        q_load.wait()

    @pl.when(relays)
    def _():
        with region("rimpass"):
            remote(rimrel, rimrel, rel_send, rel_recv, s).wait_recv()
            rim_pass().start()

    @pl.when(s == 0)
    def _():
        kbuf[:, :, :OFF] = jnp.zeros((requests, heads, OFF, hd), kbuf.dtype)
        vbuf[:, :, :OFF] = jnp.zeros((requests, heads, OFF, hd), vbuf.dtype)

    def a_remote(v, x):
        kk, r, y = v // 4, lax.rem(v, 2), lax.rem(v // 2, 2)
        return remote(
            stage.at[v, x],
            act.at[h * 2 + kk, r, me],
            a_send.at[v, x],
            a_recv.at[kk, r, me],
            z * B + y * 2 + x,
        )

    def a_local(kk, r, v):
        return pltpu.make_async_copy(
            stage.at[v, lax.rem(me, 2)], act.at[h * 2 + kk, r, me], a_loc.at[kk, r]
        )

    def a_relay(kk, r):
        return remote(
            act.at[h * 2 + kk, r], act.at[h * 2 + kk, r], p_send.at[kk, r], p_recv.at[kk, r]
        )

    def a_gather(kk, r):
        a_local(kk, r, kk * 4 + (me // 2) * 2 + r).wait()
        for o in range(1, B):
            source = lax.rem(me + o, B)
            remote(
                stage.at[0, 0],
                act.at[h * 2 + kk, r, source],
                a_send.at[0, 0],
                a_recv.at[kk, r, source],
                s,
            ).wait_recv()
        a_relay(kk, r).start()

    def unit(u, carry):
        r, k = u // heads, lax.rem(u, heads)
        v = k * 2 + r

        @pl.when((k == 0) & (s > 0))
        def _():
            with region("rimwait"):
                for which in range(2):
                    p = r * 2 + which
                    remote(rimraw.at[p], rimraw.at[p], rim_send.at[p], rim_recv.at[p], s).wait_recv()
            kbuf[r, :, :OFF] = jnp.swapaxes(rimraw[r * 2], 0, 1)
            vbuf[r, :, :OFF] = jnp.swapaxes(rimraw[r * 2 + 1], 0, 1)

        with region("att"):
            qbuf[...] = jnp.swapaxes(qraw[r, :, k], 0, 1)
            for g in range(G):
                scores = (
                    lax.dot_general(
                        qbuf[g],
                        kbuf[r, k],
                        (((1,), (1,)), ((), ())),
                        preferred_element_type=f32,
                    )
                    * inv_root
                    + bias[r]
                )
                weights = jnp.exp(scores - jnp.max(scores, axis=-1, keepdims=True))
                total = jnp.sum(weights, axis=-1, keepdims=True)
                out = jnp.dot(weights.astype(bf16), vbuf[r, k], preferred_element_type=f32)
                at = (g % 4) * hd
                stage[v, g // 4, :, at : at + hd] = (out / total).astype(bf16)
        for x in range(2):
            member = lax.rem(k, 2) * 2 + x

            @pl.when(member == me)
            def _():
                a_local(k // 2, r, v).start()

            @pl.when(member != me)
            def _(x=x):
                a_remote(v, x).start()

        with region("relay"):

            @pl.when(u < CH)
            def _():
                w_relay(1, u)

            @pl.when(u >= 2 * heads - CH + 1)
            def _():
                w_relay(2, u - (2 * heads - CH + 1))

            @pl.when(u == heads + 1)
            def _():
                a_gather(0, 0)

            @pl.when(u == heads + 3)
            def _():
                a_gather(1, 0)

        return carry

    lax.fori_loop(0, 2 * heads, unit, 0)
    with region("gather"):
        a_gather(0, 1)
        w_relay(2, CH - 1)
        a_gather(1, 1)
        for kk in range(2):
            for r in range(requests):
                a_relay(kk, r).wait_recv()

    def p_copy(c, to, frm):
        return remote(
            psend.at[to, c], precv.at[frm, c], s_send.at[to, c], s_recv.at[frm, c], z * B + to
        )

    slot_row = lax.broadcasted_iota(jnp.int32, (nb, width), 0)

    def finish(c):
        with region("finish"):
            for o in range(1, B):
                source = lax.rem(me + o, B)
                p_copy(c, source, source).wait_recv()
        total = own[c]
        for o in range(1, B):
            total += precv[lax.rem(me + o, B), c].astype(f32)
        out_ref = (bk_ref, bv_ref)[c // (CH // 2)]
        at = (c % (CH // 2)) * width
        for r in range(requests):
            live = (slot_row + 1) * ratio_ref[r, s] <= interval
            out_ref[r * nb : (r + 1) * nb, at : at + width] = jnp.where(
                live, total[r * nb : (r + 1) * nb], 0.0
            ).astype(bf16)

    for c in range(CH):
        with region(f"wwait{c}"):
            w_wait(c)

        def product(o, carry, c=c):
            to = lax.rem(me + 1 + o, B)
            total = jnp.zeros((requests * nb, width), f32)
            for zi in range(depth):
                total += jnp.dot(
                    act[zi, :, to].reshape(requests * nb, act.shape[4]),
                    wbuf[zi, c],
                    preferred_element_type=f32,
                )

            @pl.when(o < B - 1)
            def _():
                psend[to, c] = total.astype(bf16)
                p_copy(c, to, me).start()

            @pl.when(o == B - 1)
            def _():
                own[c] = total

            return carry

        with region("prod"):
            lax.fori_loop(0, B, product, 0)
        if c > 0:
            finish(c - 1)
    finish(CH - 1)

    res = rk_ref.shape[2]
    qrows = dq_ref.shape[1]
    cells = res + nb + OFF
    row_request = lax.rem(lax.broadcasted_iota(jnp.int32, (qrows, cells), 0), requests)
    cell = lax.broadcasted_iota(jnp.int32, (qrows, cells), 1)
    last = jnp.where(s == n - 1, 1, 0)
    share = G * heads // n
    with region("decode"):
        masks = []
        for r in range(requests):
            usable = (
                (cell < rlen_ref[r, s])
                | (
                    (cell >= res)
                    & (cell < res + nb)
                    & ((cell - res + 1) * ratio_ref[r, s] <= interval)
                )
                | ((cell >= res + nb + OFF - phase_ref[r] * last) & (cell >= res + nb))
            )
            masks.append(usable & (row_request == r))
        for k in range(heads):
            lanes = slice(k * hd, (k + 1) * hd)
            pieces = []
            for r in range(requests):
                keys = (
                    rk_ref[r, k],
                    bk_ref[r * nb : (r + 1) * nb, lanes],
                    kbuf[r, k, rows - OFF :],
                )
                scores = jnp.concatenate(
                    [
                        lax.dot_general(
                            dq_ref[k], key, (((1,), (1,)), ((), ())), preferred_element_type=f32
                        )
                        for key in keys
                    ],
                    axis=1,
                )
                pieces.append(jnp.where(masks[r], scores * inv_root, masked_score))
            peak = jnp.maximum(
                jnp.max(pieces[0], axis=-1, keepdims=True),
                jnp.max(pieces[1], axis=-1, keepdims=True),
            )
            total = jnp.zeros((qrows, 1), f32)
            out = jnp.zeros((qrows, hd), f32)
            for r in range(requests):
                weights = jnp.exp(pieces[r] - peak)
                total += jnp.sum(weights, axis=-1, keepdims=True)
                low = weights.astype(bf16)
                out += jnp.dot(low[:, :res], rv_ref[r, k], preferred_element_type=f32)
                out += jnp.dot(
                    low[:, res : res + nb],
                    bv_ref[r * nb : (r + 1) * nb, lanes],
                    preferred_element_type=f32,
                )
                out += jnp.dot(
                    low[:, res + nb :], vbuf[r, k, rows - OFF :], preferred_element_type=f32
                )
            lane = lax.broadcasted_iota(jnp.int32, (qrows, hd), 1)
            slots = hd // (2 * share)
            stats = jnp.where(lax.rem(lane // slots, 2) == 0, peak, total)
            stats = stats.reshape(G // share, share, pair, hd)
            lane = lax.broadcasted_iota(jnp.int32, (G // share, pair, hd), 2)
            packed = stats[:, 0]
            for j in range(1, share):
                packed = jnp.where(lane >= 2 * slots * j, stats[:, j], packed)
            dests = slice(k * G // share, (k + 1) * G // share)
            snd[dests] = out.reshape(G // share, share * pair, hd).astype(bf16)
            snd_stats[dests] = packed

    def d_copy(to, frm):
        return remote(snd.at[to], rcv.at[frm], d_send.at[to], d_recv.at[frm], to)

    def e_copy(to, frm):
        return remote(snd_stats.at[to], rcv_stats.at[frm], e_send.at[to], e_recv.at[frm], to)

    def t_copy(to, frm):
        return remote(att.at[frm], att.at[frm], t_send.at[to], t_recv.at[frm], to)

    for o in range(1, n):
        e_copy(lax.rem(s + o, n), s).start()
        d_copy(lax.rem(s + o, n), s).start()
    rcv[s] = snd[s]
    rcv_stats[s] = snd_stats[s]

    with region("outs"):
        for made, out_ref in ((bk_ref, bk_out), (bv_ref, bv_out)):
            by_head = jnp.stack([made[:, k * hd : (k + 1) * hd] for k in range(heads)], axis=0)
            out_ref[...] = jnp.swapaxes(by_head, 0, 1)

    with region("drain"):
        for c in range(CH):
            for o in range(1, B):
                p_copy(c, lax.rem(me + o, B), me).wait_send()
        for kk in range(2):
            for r in range(requests):
                a_relay(kk, r).wait_send()
        for v in range(2 * heads):
            for x in range(2):

                @pl.when((v // 2 % 2) * 2 + x != me)
                def _(v=v, x=x):
                    a_remote(jnp.int32(v), x).wait_send()

        for way in range(2):
            for d in range(depth - 1):
                shard, target, there = w_out(way, d)

                @pl.when(there)
                def _(way=way, d=d, shard=shard, target=target):
                    for c in range(CH):
                        w_copy(way, d, c, shard, target).wait_send()

        @pl.when(me < B - 1)
        def _():
            for p in range(2 * requests):
                rim_near(p).wait_send()

        @pl.when(crosses)
        def _():
            rim_near(0).wait_send()
            for p in range(1, 2 * requests):
                rim_far(p).wait_send()

        @pl.when(relays)
        def _():
            rim_pass().wait_send()

    with region("dwait"):
        for o in range(1, n):
            source = lax.rem(s + o, n)
            e_copy(source, source).wait_recv()
            d_copy(source, source).wait_recv()
    landed = rcv[...].astype(f32)
    attended = []
    for j in range(share):
        at = 2 * slots * j
        peaks = rcv_stats[:, :, at : at + 1]
        sums = rcv_stats[:, :, at + slots : at + slots + 1]
        scale = jnp.exp(peaks - jnp.max(peaks, axis=0, keepdims=True))
        mixed = jnp.sum(scale * landed[:, j * pair : (j + 1) * pair], axis=0)
        attended.append(mixed / jnp.sum(scale * sums, axis=0))
    att[s] = jnp.concatenate(attended, axis=0).astype(bf16)
    for o in range(1, n):
        t_copy(lax.rem(s + o, n), s).start()
    ow_load.wait()
    with region("twait"):
        for o in range(1, n):
            d_copy(lax.rem(s + o, n), s).wait_send()
            e_copy(lax.rem(s + o, n), s).wait_send()
        for o in range(1, n):
            source = lax.rem(s + o, n)
            t_copy(source, source).wait_recv()
    wide = [att[i].astype(f32) for i in range(n)]
    vectors = jnp.concatenate(
        [wide[i][j * pair : (j + 1) * pair] for i in range(n) for j in range(share)], axis=1
    ).astype(bf16)
    with region("outproj"):
        partial_value = jnp.dot(vectors, owbuf[...], preferred_element_type=f32)
        part[0] = partial_value
    swap = remote(part.at[0], part.at[1], h_send, h_recv)
    swap.start()
    with region("swap"):
        for o in range(1, n):
            t_copy(lax.rem(s + o, n), s).wait_send()
        swap.wait_recv()
    first = jnp.where(h == 0, part[0], part[1])
    second = jnp.where(h == 0, part[1], part[0])
    summed = (first + second).astype(bf16)
    for t in range(steps):
        proj_ref[t] = summed[t * requests : (t + 1) * requests]
    swap.wait_send()


def fused_body(
    shard_count,
    raw_keys,
    raw_values,
    phase,
    ratio,
    resident_len,
    beacon_queries,
    beacon_wk,
    beacon_wv,
    resident_keys,
    resident_values,
    decode_queries,
    out_weight,
):
    n = shard_count
    depth = n // B
    requests, interval, heads, hd = raw_keys.shape
    steps = decode_queries.shape[0]
    nb = beacon_queries.shape[1]
    rows = interval + OFF
    res = resident_keys.shape[1]
    feature, columns = beacon_wk.shape
    width = 2 * columns // CH
    pair = requests * steps
    share = G * heads // n
    bf16, f32 = jnp.bfloat16, jnp.float32
    dma = pltpu.SemaphoreType.DMA
    smem = pl.BlockSpec(memory_space=pltpu.SMEM)
    anywhere = pl.BlockSpec(memory_space=pl.ANY)
    vmem = pl.BlockSpec(memory_space=pltpu.VMEM)
    keys, values, projected = pl.pallas_call(
        functools.partial(fused_kernel, n),
        out_shape=(
            jax.ShapeDtypeStruct((requests * nb, heads, hd), bf16),
            jax.ShapeDtypeStruct((requests * nb, heads, hd), bf16),
            jax.ShapeDtypeStruct((steps, requests, out_weight.shape[1]), bf16),
        ),
        in_specs=[smem] * 3 + [anywhere] * 9,
        out_specs=(vmem, vmem, vmem),
        scratch_shapes=[
            pltpu.VMEM(raw_keys.shape, bf16),
            pltpu.VMEM(raw_values.shape, bf16),
            pltpu.VMEM(beacon_queries.shape, bf16),
            pltpu.VMEM(resident_keys.shape, bf16),
            pltpu.VMEM(resident_values.shape, bf16),
            pltpu.VMEM(decode_queries.shape, bf16),
            pltpu.VMEM((2 * requests, OFF, heads, hd), bf16),
            pltpu.VMEM((OFF, heads, hd), bf16),
            pltpu.VMEM((requests, heads, rows, hd), bf16),
            pltpu.VMEM((requests, heads, rows, hd), bf16),
            pltpu.VMEM((G, nb, hd), bf16),
            pltpu.VMEM((depth, CH, feature, width), bf16),
            pltpu.VMEM((depth, requests, B, nb, feature), bf16),
            pltpu.VMEM((requests * heads, 2, nb, feature), bf16),
            pltpu.VMEM((B, CH, requests * nb, width), bf16),
            pltpu.VMEM((B, CH, requests * nb, width), bf16),
            pltpu.VMEM((CH, requests * nb, width), f32),
            pltpu.VMEM((requests, nb, rows), f32),
            pltpu.VMEM(out_weight.shape, bf16),
            pltpu.VMEM((requests, heads, res, hd), bf16),
            pltpu.VMEM((requests, heads, res, hd), bf16),
            pltpu.VMEM((heads, G * pair, hd), bf16),
            pltpu.VMEM((requests * nb, columns), bf16),
            pltpu.VMEM((requests * nb, columns), bf16),
            pltpu.VMEM((n, share * pair, hd), bf16),
            pltpu.VMEM((n, pair, hd), f32),
            pltpu.VMEM((n, share * pair, hd), bf16),
            pltpu.VMEM((n, pair, hd), f32),
            pltpu.VMEM((n, share * pair, hd), bf16),
            pltpu.VMEM((2, pair, out_weight.shape[1]), f32),
            dma((CH + 2 * requests + 5,)),
            dma((2 * requests,)),
            dma((2 * requests,)),
            dma,
            dma,
            dma((2, depth - 1, CH)),
            dma((2, depth - 1, CH)),
            dma((requests * heads, 2)),
            dma((2, requests, B)),
            dma((2, requests)),
            dma((2, requests)),
            dma((2, requests)),
            dma((B, CH)),
            dma((B, CH)),
            dma((n,)),
            dma((n,)),
            dma((n,)),
            dma((n,)),
            dma((n,)),
            dma((n,)),
            dma,
            dma,
        ],
        compiler_params=pltpu.CompilerParams(
            collective_id=0, has_side_effects=True, vmem_limit_bytes=60 * 1024 * 1024
        ),
    )(
        phase,
        ratio,
        resident_len,
        raw_keys,
        raw_values,
        beacon_queries,
        beacon_wk,
        beacon_wv,
        resident_keys,
        resident_values,
        decode_queries,
        out_weight,
    )
    return (
        keys.reshape(requests, nb, heads, hd),
        values.reshape(requests, nb, heads, hd),
        projected,
    )


def chosen_body(shard_count, head_count):
    def run(*arrays):
        requests, _, heads, hd = arrays[0].shape
        feature = arrays[6].shape[0]
        fits = (
            head_count == 2
            and shard_count == B * B
            and requests == 2
            and heads == B
            and 2 * feature == G * hd
        )
        return fused_body(shard_count, *arrays) if fits else body(*arrays)

    return run


def solution(mesh):
    return jax.shard_map(
        chosen_body(mesh.shape["seq"], mesh.shape["head"]),
        mesh=mesh,
        in_specs=(
            P(None, "seq", "head", None),
            P(None, "seq", "head", None),
            P(),
            P(),
            P(),
            P(None, "seq", "head", None, None),
            P("seq", "head"),
            P("seq", "head"),
            P(None, "seq", "head", None),
            P(None, "seq", "head", None),
            P(None, None, "head", None, None),
            P("head", "seq"),
        ),
        out_specs=(
            P(None, "seq", "head", None),
            P(None, "seq", "head", None),
            P(None, None, "seq"),
        ),
        check_vma=False,
    )
```

time: 137 us -> 120 us (0.88)
  local copies, waits for them, and re-layouts: 12.8 us -> 4.79 us
  Pallas kernels: 123 us -> 115 us
    pallas_call x1, Pallas kernels: 123 us -> 115 us  [fused_body(): pl.pallas_call(functools.partial(fused_kernel, n), out_shape=(jax.ShapeDt...]
    reshape x4 -> x0, local copies, waits for them, and re-layouts: 4.75 us -> none  [the longest x1 1.72 us: fused_body(): keys.reshape(requests, nb, heads, hd)]
    transpose x2 -> x0, local copies, waits for them, and re-layouts: 4.21 us -> none  [the longest x1 2.69 us: fused_body(): jnp.transpose(raw_values, by_head)]
    unnamed x5 -> x3, local copies, waits for them, and re-layouts: 3.88 us -> 4.79 us
where the time goes in v1:
time: 120 us
  Pallas kernels  115 us (96%)
  local copies, waits for them, and re-layouts  4.79 us (4%)
    pallas_call x1, Pallas kernels, fused_body(): pl.pallas_call(functools.partial(fused_kernel, n), out_shape=(jax.ShapeDt...  115 us
    unnamed x3, local copies, waits for them, and re-layouts  4.79 us

profile of v1, /device:TPU:0, one launch (start us, length us, event | category | flops | bytes accessed | tf_op | source)
XLA Modules:
  0.0 119.9 jit_solution(1164831929426731797)
XLA Ops:
  0.6 114.5 %shard_map.139 = (bf16[256,4,128]{2,1,0:T(4,128)(2,1)}, bf16[256,4,128]{2,1,0:T(4,128)(2,1)}, bf16[4,2,512]{2,1,0:T(2,128)(2,1)}) custom-call(s32[2]{0:T(128)} %phase_ref.1, s32[2,16]{1,0:T(2,128)} %ratio_ref.1, s32[2,16]{1,0:T(2,128)} %rlen_ref.1, bf16[2,1024,4,128]{3,2,1,0:T(4,128)(2,1)} %k_hbm.1, bf16[2,1024,4,128]{3,2,1,0:T(4,128)(2,1)} %v_hbm.1, ...), custom_call_target="tpu_custom_call" | custom-call | tf_op jit(solution)/shard_map/pallas_call | solution.py:784
  115.2 1.7 %copy.18 = bf16[2,128,4,128]{3,2,1,0:T(4,128)(2,1)} copy(bf16[2,128,4,128]{3,2,1,0:T(4,128)(2,1)} %bitcast.3) | data formatting | bytes 524288
  116.9 1.7 %copy.19 = bf16[2,128,4,128]{3,2,1,0:T(4,128)(2,1)} copy(bf16[2,128,4,128]{3,2,1,0:T(4,128)(2,1)} %bitcast.2) | data formatting | bytes 524288
  118.6 1.3 %copy.20 = bf16[4,2,512]{2,1,0:T(2,128)(2,1)} copy(bf16[4,2,512]{2,1,0:T(2,128)(2,1)} %get-tuple-element.14) | data formatting | bytes 16384

commit v2 on v1

--- a/solution.py
+++ b/solution.py
@@ -190,7 +190,7 @@
     ow_hbm,
     bk_out,
     bv_out,
-    proj_ref,
+    proj_out,
     kraw,
     vraw,
     qraw,
@@ -221,7 +221,11 @@
     rcv_stats,
     att,
     part,
+    bk_rows,
+    bv_rows,
+    proj_rows,
     load_sem,
+    out_sem,
     rim_send,
     rim_recv,
     rel_send,
@@ -313,10 +317,10 @@
 
     def rim_far(p):
         source = (k_hbm, v_hbm)[p % 2].at[p // 2, interval - OFF :]
-        return remote(source, rimrel, rim_send.at[p], rel_recv, z * B + B - 1 - p)
+        return remote(source, rimrel, rim_send.at[p], rel_recv, z * B + lax.rem(p, B - 1))
 
     def rim_pass():
-        p = B - 1 - me
+        p = jnp.where(me == 0, B - 1, me)
         return remote(rimrel, rimraw.at[p], rel_send, rim_recv.at[p], lax.rem((z + 1) * B, n))
 
     @pl.when(me < B - 1)
@@ -378,9 +382,24 @@
                 def _(way=way, d=d, shard=shard):
                     w_copy(way, d, c, shard, z).wait_recv()
 
-    with region("w_own"):
-        for c in range(CH):
-            w_own(c)
+    def rim_relay():
+        with region("rimpass"):
+            remote(rimrel, rimrel, rel_send, rel_recv, s).wait_recv()
+            rim_pass().start()
+
+    w_own(0)
+
+    @pl.when(me != 1)
+    def _():
+        w_own(1)
+
+    @pl.when((me == 0) | (me == B - 1))
+    def _():
+        w_own(2)
+
+    @pl.when(me == B - 1)
+    def _():
+        w_own(3)
 
     with region("prep"):
         for r in range(requests):
@@ -407,11 +426,18 @@
             dq_ref[k] = jnp.swapaxes(asked, 0, 1).reshape(G * pair, hd).astype(bf16)
         q_load.wait()
 
-    @pl.when(relays)
+    @pl.when(relays & (me != 0))
     def _():
-        with region("rimpass"):
-            remote(rimrel, rimrel, rel_send, rel_recv, s).wait_recv()
-            rim_pass().start()
+        rim_relay()
+
+    @pl.when(me == 1)
+    def _():
+        w_own(1)
+
+    @pl.when((me == 1) | (me == 2))
+    def _():
+        w_own(2)
+        w_own(3)
 
     @pl.when(s == 0)
     def _():
@@ -494,6 +520,14 @@
                 a_remote(v, x).start()
 
         with region("relay"):
+
+            @pl.when((u == 0) & (me == 0))
+            def _():
+                @pl.when(relays)
+                def _():
+                    rim_relay()
+
+                w_own(3)
 
             @pl.when(u < CH)
             def _():
@@ -662,9 +696,14 @@
     rcv_stats[s] = snd_stats[s]
 
     with region("outs"):
-        for made, out_ref in ((bk_ref, bk_out), (bv_ref, bv_out)):
+        outs = []
+        for i, (made, made_rows, out) in enumerate(
+            ((bk_ref, bk_rows, bk_out), (bv_ref, bv_rows, bv_out))
+        ):
             by_head = jnp.stack([made[:, k * hd : (k + 1) * hd] for k in range(heads)], axis=0)
-            out_ref[...] = jnp.swapaxes(by_head, 0, 1)
+            made_rows[...] = jnp.swapaxes(by_head, 0, 1)
+            outs.append(pltpu.make_async_copy(made_rows, out, out_sem.at[i]))
+            outs[-1].start()
 
     with region("drain"):
         for c in range(CH):
@@ -746,8 +785,19 @@
     second = jnp.where(h == 0, part[1], part[0])
     summed = (first + second).astype(bf16)
     for t in range(steps):
-        proj_ref[t] = summed[t * requests : (t + 1) * requests]
+        proj_rows[t] = summed[t * requests : (t + 1) * requests]
+    outs.append(pltpu.make_async_copy(proj_rows, proj_out, out_sem.at[2]))
+    outs[-1].start()
     swap.wait_send()
+    with region("outwait"):
+        for copy in outs:
+            copy.wait()
+
+
+def handed_on(keys_ref, values_ref, projected_ref, keys_out, values_out, projected_out):
+    keys_out[...] = keys_ref[...]
+    values_out[...] = values_ref[...]
+    projected_out[...] = projected_ref[...]
 
 
 def fused_body(
@@ -789,7 +839,7 @@
             jax.ShapeDtypeStruct((steps, requests, out_weight.shape[1]), bf16),
         ),
         in_specs=[smem] * 3 + [anywhere] * 9,
-        out_specs=(vmem, vmem, vmem),
+        out_specs=(anywhere, anywhere, anywhere),
         scratch_shapes=[
             pltpu.VMEM(raw_keys.shape, bf16),
             pltpu.VMEM(raw_values.shape, bf16),
@@ -821,7 +871,11 @@
             pltpu.VMEM((n, pair, hd), f32),
             pltpu.VMEM((n, share * pair, hd), bf16),
             pltpu.VMEM((2, pair, out_weight.shape[1]), f32),
+            pltpu.VMEM((requests * nb, heads, hd), bf16),
+            pltpu.VMEM((requests * nb, heads, hd), bf16),
+            pltpu.VMEM((steps, requests, out_weight.shape[1]), bf16),
             dma((CH + 2 * requests + 5,)),
+            dma((3,)),
             dma((2 * requests,)),
             dma((2 * requests,)),
             dma,
@@ -861,6 +915,12 @@
         decode_queries,
         out_weight,
     )
+    keys, values, projected = pl.pallas_call(
+        handed_on,
+        out_shape=tuple(jax.ShapeDtypeStruct(x.shape, x.dtype) for x in (keys, values, projected)),
+        in_specs=[vmem] * 3,
+        out_specs=(vmem,) * 3,
+    )(keys, values, projected)
     return (
         keys.reshape(requests, nb, heads, hd),
         values.reshape(requests, nb, heads, hd),

time: 120 us -> 111 us (0.925)
  Pallas kernels: 115 us -> 110 us
  local copies, waits for them, and re-layouts: 4.79 us -> 0 us
    pallas_call x1, Pallas kernels: 115 us -> 108 us  [fused_body(): pl.pallas_call(functools.partial(fused_kernel, n), out_shape=(jax.ShapeDt...]
    unnamed x3 -> x0, local copies, waits for them, and re-layouts: 4.79 us -> none
    pallas_call x0 -> x1, Pallas kernels: none -> 1.84 us  [fused_body(): pl.pallas_call(handed_on, out_shape=tuple((jax.ShapeDtypeStruct(x.shape,...]
where the time goes in v2:
time: 111 us
  Pallas kernels  110 us (99%)
    pallas_call x1, Pallas kernels, fused_body(): pl.pallas_call(functools.partial(fused_kernel, n), out_shape=(jax.ShapeDt...  108 us

profile of v2, /device:TPU:0, one launch (start us, length us, event | category | flops | bytes accessed | tf_op | source)
XLA Modules:
  0.0 110.7 jit_solution(12405713587729548342)
XLA Ops:
  0.6 108.2 %shard_map.139 = (bf16[256,4,128]{2,1,0:T(4,128)(2,1)}, bf16[256,4,128]{2,1,0:T(4,128)(2,1)}, bf16[4,2,512]{2,1,0:T(2,128)(2,1)}) custom-call(s32[2]{0:T(128)} %phase_ref.1, s32[2,16]{1,0:T(2,128)} %ratio_ref.1, s32[2,16]{1,0:T(2,128)} %rlen_ref.1, bf16[2,1024,4,128]{3,2,1,0:T(4,128)(2,1)} %k_hbm.1, bf16[2,1024,4,128]{3,2,1,0:T(4,128)(2,1)} %v_hbm.1, ...), custom_call_target="tpu_custom_call" | custom-call | tf_op jit(solution)/shard_map/pallas_call | solution.py:834
  108.9 1.8 %shard_map.140 = (bf16[256,4,128]{2,1,0:T(4,128)(2,1)}, bf16[256,4,128]{2,1,0:T(4,128)(2,1)}, bf16[4,2,512]{2,1,0:T(2,128)(2,1)}) custom-call(bf16[256,4,128]{2,1,0:T(4,128)(2,1)} %get-tuple-element.9.keys_ref, bf16[256,4,128]{2,1,0:T(4,128)(2,1)} %get-tuple-element.10.values_ref, bf16[4,2,512]{2,1,0:T(2,128)(2,1)} %get-tuple-element.11.projected_ref), custom_call_target="tpu_custom_call" | custom-call | tf_op jit(solution)/shard_map/pallas_call | solution.py:918

commit v3 on v2

--- a/solution.py
+++ b/solution.py
@@ -171,7 +171,6 @@
 
 
 B = 4
-CH = 4
 
 
 def fused_kernel(
@@ -190,7 +189,7 @@
     ow_hbm,
     bk_out,
     bv_out,
-    proj_out,
+    part_out,
     kraw,
     vraw,
     qraw,
@@ -215,6 +214,8 @@
     dq_ref,
     bk_ref,
     bv_ref,
+    dacc,
+    dlow,
     snd,
     snd_stats,
     rcv,
@@ -223,8 +224,8 @@
     part,
     bk_rows,
     bv_rows,
-    proj_rows,
     load_sem,
+    w_load,
     out_sem,
     rim_send,
     rim_recv,
@@ -257,7 +258,8 @@
     requests, interval, heads, hd = kraw.shape
     rows = interval + OFF
     nb = bias.shape[1]
-    width = wbuf.shape[3]
+    blocks = wbuf.shape[1]
+    units = [(b, 2) for b in range(0, blocks - 2, 2)] + [(blocks - 2, 1), (blocks - 1, 1)]
     inv_root = 1.0 / math.sqrt(hd)
     f32 = jnp.float32
     bf16 = jnp.bfloat16
@@ -273,6 +275,12 @@
             device_id_type=pl.DeviceIdType.MESH,
         )
 
+    def got(ref, sem):
+        remote(ref, ref, sem, sem, s).wait_recv()
+
+    def sent(ref, sem):
+        remote(ref, ref, sem, sem, s).wait_send()
+
     loads = []
 
     def load(source, target):
@@ -280,12 +288,10 @@
         loads[-1].start()
         return loads[-1]
 
-    half = wk_hbm.shape[1] // (CH // 2)
-    w_load = []
-    for c in range(CH):
-        source = (wk_hbm, wv_hbm)[c // (CH // 2)]
-        first = (c % (CH // 2)) * half
-        w_load.append(load(source.at[:, first : first + half], wbuf.at[z, c]))
+    for i, (b, count) in enumerate(units):
+        for at in range(b, b + count):
+            source = (wk_hbm, wv_hbm)[at // heads].at[:, (at % heads) * hd : (at % heads + 1) * hd]
+            pltpu.make_async_copy(source, wbuf.at[z, at], w_load.at[i]).start()
     kv_load = [
         load((k_hbm, v_hbm)[p % 2].at[p // 2], (kraw, vraw)[p % 2].at[p // 2])
         for p in range(2 * requests)
@@ -313,15 +319,15 @@
 
     def rim_near(p):
         source = (k_hbm, v_hbm)[p % 2].at[p // 2, interval - OFF :]
-        return remote(source, rimraw.at[p], rim_send.at[p], rim_recv.at[p], lax.rem(s + 1, n))
+        return remote(source, rimraw.at[p], rim_send, rim_recv.at[p // 2], lax.rem(s + 1, n))
 
     def rim_far(p):
         source = (k_hbm, v_hbm)[p % 2].at[p // 2, interval - OFF :]
-        return remote(source, rimrel, rim_send.at[p], rel_recv, z * B + lax.rem(p, B - 1))
+        return remote(source, rimrel, rim_send, rel_recv, z * B + lax.rem(p, B - 1))
 
     def rim_pass():
         p = jnp.where(me == 0, B - 1, me)
-        return remote(rimrel, rimraw.at[p], rel_send, rim_recv.at[p], lax.rem((z + 1) * B, n))
+        return remote(rimrel, rimraw.at[p], rel_send, rim_recv.at[p // 2], lax.rem((z + 1) * B, n))
 
     @pl.when(me < B - 1)
     def _():
@@ -334,12 +340,13 @@
         for p in range(1, 2 * requests):
             rim_far(p).start()
 
-    def w_copy(way, d, c, shard, target):
+    def w_copy(way, d, i, shard, target):
+        b, count = units[i]
         return remote(
-            wbuf.at[shard, c],
-            wbuf.at[shard, c],
-            w_send.at[way, d, c],
-            w_recv.at[way, d, c],
+            wbuf.at[shard, b : b + count],
+            wbuf.at[shard, b : b + count],
+            w_send.at[way, d],
+            w_recv.at[way, d, i],
             target * B + me,
         )
 
@@ -353,25 +360,29 @@
             return z - 1 - d, z - 1 - d >= 0
         return z + 1 + d, z + 1 + d < depth
 
-    def w_own(c):
-        w_load[c].wait()
-        for way in range(2):
-            shard, target, there = w_out(way, 0)
-
-            @pl.when(there)
-            def _(way=way, shard=shard, target=target):
-                w_copy(way, 0, c, shard, target).start()
-
-    def w_relay(d, c):
+    def w_own(first, end):
+        for i in range(first, end):
+            b, count = units[i]
+            pltpu.make_async_copy(
+                wbuf.at[z, b : b + count], wbuf.at[z, b : b + count], w_load.at[i]
+            ).wait()
+            for way in range(2):
+                shard, target, there = w_out(way, 0)
+
+                @pl.when(there)
+                def _(way=way, i=i, shard=shard, target=target):
+                    w_copy(way, 0, i, shard, target).start()
+
+    def w_relay(d, i):
         for way in range(2):
             shard, target, onward = w_out(way, d)
 
             @pl.when(onward)
             def _(way=way, shard=shard, target=target):
-                w_copy(way, d - 1, c, shard, z).wait_recv()
-                w_copy(way, d, c, shard, target).start()
-
-    def w_wait(c):
+                w_copy(way, d - 1, i, shard, z).wait_recv()
+                w_copy(way, d, i, shard, target).start()
+
+    def w_wait(i):
         for way in range(2):
             for d in range(depth - 1):
                 shard, there = w_in(way, d)
@@ -380,26 +391,22 @@
 
                 @pl.when(there)
                 def _(way=way, d=d, shard=shard):
-                    w_copy(way, d, c, shard, z).wait_recv()
+                    w_copy(way, d, i, shard, z).wait_recv()
 
     def rim_relay():
         with region("rimpass"):
-            remote(rimrel, rimrel, rel_send, rel_recv, s).wait_recv()
+            got(rimrel, rel_recv)
             rim_pass().start()
 
-    w_own(0)
+    w_own(0, 1)
 
     @pl.when(me != 1)
     def _():
-        w_own(1)
+        w_own(1, 2)
 
     @pl.when((me == 0) | (me == B - 1))
     def _():
-        w_own(2)
-
-    @pl.when(me == B - 1)
-    def _():
-        w_own(3)
+        w_own(2, len(units))
 
     with region("prep"):
         for r in range(requests):
@@ -432,12 +439,11 @@
 
     @pl.when(me == 1)
     def _():
-        w_own(1)
+        w_own(1, 2)
 
     @pl.when((me == 1) | (me == 2))
     def _():
-        w_own(2)
-        w_own(3)
+        w_own(2, len(units))
 
     @pl.when(s == 0)
     def _():
@@ -449,8 +455,8 @@
         return remote(
             stage.at[v, x],
             act.at[h * 2 + kk, r, me],
-            a_send.at[v, x],
-            a_recv.at[kk, r, me],
+            a_send,
+            a_recv.at[kk, r],
             z * B + y * 2 + x,
         )
 
@@ -461,20 +467,12 @@
 
     def a_relay(kk, r):
         return remote(
-            act.at[h * 2 + kk, r], act.at[h * 2 + kk, r], p_send.at[kk, r], p_recv.at[kk, r]
+            act.at[h * 2 + kk, r], act.at[h * 2 + kk, r], p_send, p_recv
         )
 
     def a_gather(kk, r):
         a_local(kk, r, kk * 4 + (me // 2) * 2 + r).wait()
-        for o in range(1, B):
-            source = lax.rem(me + o, B)
-            remote(
-                stage.at[0, 0],
-                act.at[h * 2 + kk, r, source],
-                a_send.at[0, 0],
-                a_recv.at[kk, r, source],
-                s,
-            ).wait_recv()
+        got(act.at[0, 0, : B - 1], a_recv.at[kk, r])
         a_relay(kk, r).start()
 
     def unit(u, carry):
@@ -484,9 +482,7 @@
         @pl.when((k == 0) & (s > 0))
         def _():
             with region("rimwait"):
-                for which in range(2):
-                    p = r * 2 + which
-                    remote(rimraw.at[p], rimraw.at[p], rim_send.at[p], rim_recv.at[p], s).wait_recv()
+                got(rimraw.at[:2], rim_recv.at[r])
             kbuf[r, :, :OFF] = jnp.swapaxes(rimraw[r * 2], 0, 1)
             vbuf[r, :, :OFF] = jnp.swapaxes(rimraw[r * 2 + 1], 0, 1)
 
@@ -521,21 +517,21 @@
 
         with region("relay"):
 
-            @pl.when((u == 0) & (me == 0))
+            for i in range(len(units)):
+
+                @pl.when(u == min(i, heads - 1))
+                def _(i=i):
+                    w_relay(1, i)
+
+            @pl.when((u == 0) & (me == 0) & relays)
             def _():
-                @pl.when(relays)
-                def _():
-                    rim_relay()
-
-                w_own(3)
-
-            @pl.when(u < CH)
-            def _():
-                w_relay(1, u)
-
-            @pl.when(u >= 2 * heads - CH + 1)
-            def _():
-                w_relay(2, u - (2 * heads - CH + 1))
+                rim_relay()
+
+            for i in range(len(units) - 2):
+
+                @pl.when(u == heads + 1 + i)
+                def _(i=i):
+                    w_relay(2, i)
 
             @pl.when(u == heads + 1)
             def _():
@@ -550,74 +546,91 @@
     lax.fori_loop(0, 2 * heads, unit, 0)
     with region("gather"):
         a_gather(0, 1)
-        w_relay(2, CH - 1)
+        w_relay(2, len(units) - 2)
+        w_relay(2, len(units) - 1)
         a_gather(1, 1)
-        for kk in range(2):
+        got(act.at[:2], p_recv)
+
+    def p_copy(i, to, frm):
+        b, count = units[i]
+        return remote(
+            psend.at[to, b : b + count], precv.at[frm, b : b + count], s_send, s_recv.at[i], z * B + to
+        )
+
+    slot_row = lax.broadcasted_iota(jnp.int32, (nb, hd), 0)
+
+    def finish(i):
+        b, count = units[i]
+        with region(f"finish{i}"):
+            got(precv.at[: B - 1, b : b + count], s_recv.at[i])
+        for at in range(b, b + count):
+            total = own[at]
+            for o in range(1, B):
+                total += precv[lax.rem(me + o, B), at].astype(f32)
+            out_ref = (bk_ref, bv_ref)[at // heads]
             for r in range(requests):
-                a_relay(kk, r).wait_recv()
-
-    def p_copy(c, to, frm):
-        return remote(
-            psend.at[to, c], precv.at[frm, c], s_send.at[to, c], s_recv.at[frm, c], z * B + to
-        )
-
-    slot_row = lax.broadcasted_iota(jnp.int32, (nb, width), 0)
-
-    def finish(c):
-        with region("finish"):
-            for o in range(1, B):
-                source = lax.rem(me + o, B)
-                p_copy(c, source, source).wait_recv()
-        total = own[c]
-        for o in range(1, B):
-            total += precv[lax.rem(me + o, B), c].astype(f32)
-        out_ref = (bk_ref, bv_ref)[c // (CH // 2)]
-        at = (c % (CH // 2)) * width
-        for r in range(requests):
-            live = (slot_row + 1) * ratio_ref[r, s] <= interval
-            out_ref[r * nb : (r + 1) * nb, at : at + width] = jnp.where(
-                live, total[r * nb : (r + 1) * nb], 0.0
-            ).astype(bf16)
-
-    for c in range(CH):
-        with region(f"wwait{c}"):
-            w_wait(c)
-
-        def product(o, carry, c=c):
+                live = (slot_row + 1) * ratio_ref[r, s] <= interval
+                out_ref[at % heads, r * nb : (r + 1) * nb] = jnp.where(
+                    live, total[r * nb : (r + 1) * nb], 0.0
+                ).astype(bf16)
+
+    def product(i):
+        b, count = units[i]
+
+        def step(o, carry):
             to = lax.rem(me + 1 + o, B)
-            total = jnp.zeros((requests * nb, width), f32)
+            total = jnp.zeros((requests * nb, count * hd), f32)
             for zi in range(depth):
                 total += jnp.dot(
                     act[zi, :, to].reshape(requests * nb, act.shape[4]),
-                    wbuf[zi, c],
+                    jnp.concatenate([wbuf[zi, at] for at in range(b, b + count)], axis=1),
                     preferred_element_type=f32,
                 )
 
             @pl.when(o < B - 1)
             def _():
-                psend[to, c] = total.astype(bf16)
-                p_copy(c, to, me).start()
+                for at in range(count):
+                    psend[to, b + at] = total[:, at * hd : (at + 1) * hd].astype(bf16)
+                p_copy(i, to, me).start()
 
             @pl.when(o == B - 1)
             def _():
-                own[c] = total
+                for at in range(count):
+                    own[b + at] = total[:, at * hd : (at + 1) * hd]
 
             return carry
 
-        with region("prod"):
-            lax.fori_loop(0, B, product, 0)
-        if c > 0:
-            finish(c - 1)
-    finish(CH - 1)
+        with region(f"prod{i}"):
+            lax.fori_loop(0, B, step, 0)
 
     res = rk_ref.shape[2]
     qrows = dq_ref.shape[1]
     cells = res + nb + OFF
-    row_request = lax.rem(lax.broadcasted_iota(jnp.int32, (qrows, cells), 0), requests)
-    cell = lax.broadcasted_iota(jnp.int32, (qrows, cells), 1)
-    last = jnp.where(s == n - 1, 1, 0)
-    share = G * heads // n
-    with region("decode"):
+    mergers = snd.shape[0]
+    share = G * heads // mergers
+    slots = hd // (2 * share)
+    per_head = G // share
+    first_merger = (depth // 2) * B - mergers // 2
+    mine = s - first_merger
+    merges = (mine >= 0) & (mine < mergers)
+
+    def e_copy(to):
+        return remote(snd_stats.at[to], rcv_stats.at[s], e_send, e_recv, first_merger + to)
+
+    def d_copy(to):
+        return remote(snd.at[to], rcv.at[s], d_send, d_recv, first_merger + to)
+
+    def to_mergers(copy, first, end):
+        for to in range(first, end):
+
+            @pl.when(mine != to)
+            def _(to=to):
+                copy(to).start()
+
+    def decode_weights():
+        row_request = lax.rem(lax.broadcasted_iota(jnp.int32, (qrows, cells), 0), requests)
+        cell = lax.broadcasted_iota(jnp.int32, (qrows, cells), 1)
+        last = jnp.where(s == n - 1, 1, 0)
         masks = []
         for r in range(requests):
             usable = (
@@ -631,12 +644,11 @@
             )
             masks.append(usable & (row_request == r))
         for k in range(heads):
-            lanes = slice(k * hd, (k + 1) * hd)
             pieces = []
             for r in range(requests):
                 keys = (
                     rk_ref[r, k],
-                    bk_ref[r * nb : (r + 1) * nb, lanes],
+                    bk_ref[k, r * nb : (r + 1) * nb],
                     kbuf[r, k, rows - OFF :],
                 )
                 scores = jnp.concatenate(
@@ -659,145 +671,148 @@
                 weights = jnp.exp(pieces[r] - peak)
                 total += jnp.sum(weights, axis=-1, keepdims=True)
                 low = weights.astype(bf16)
+                dlow[k, r] = low[:, res : res + nb]
                 out += jnp.dot(low[:, :res], rv_ref[r, k], preferred_element_type=f32)
-                out += jnp.dot(
-                    low[:, res : res + nb],
-                    bv_ref[r * nb : (r + 1) * nb, lanes],
-                    preferred_element_type=f32,
-                )
                 out += jnp.dot(
                     low[:, res + nb :], vbuf[r, k, rows - OFF :], preferred_element_type=f32
                 )
+            dacc[k] = out
             lane = lax.broadcasted_iota(jnp.int32, (qrows, hd), 1)
-            slots = hd // (2 * share)
             stats = jnp.where(lax.rem(lane // slots, 2) == 0, peak, total)
-            stats = stats.reshape(G // share, share, pair, hd)
-            lane = lax.broadcasted_iota(jnp.int32, (G // share, pair, hd), 2)
+            stats = stats.reshape(per_head, share, pair, hd)
+            lane = lax.broadcasted_iota(jnp.int32, (per_head, pair, hd), 2)
             packed = stats[:, 0]
             for j in range(1, share):
                 packed = jnp.where(lane >= 2 * slots * j, stats[:, j], packed)
-            dests = slice(k * G // share, (k + 1) * G // share)
-            snd[dests] = out.reshape(G // share, share * pair, hd).astype(bf16)
-            snd_stats[dests] = packed
-
-    def d_copy(to, frm):
-        return remote(snd.at[to], rcv.at[frm], d_send.at[to], d_recv.at[frm], to)
-
-    def e_copy(to, frm):
-        return remote(snd_stats.at[to], rcv_stats.at[frm], e_send.at[to], e_recv.at[frm], to)
-
-    def t_copy(to, frm):
-        return remote(att.at[frm], att.at[frm], t_send.at[to], t_recv.at[frm], to)
-
-    for o in range(1, n):
-        e_copy(lax.rem(s + o, n), s).start()
-        d_copy(lax.rem(s + o, n), s).start()
-    rcv[s] = snd[s]
-    rcv_stats[s] = snd_stats[s]
-
-    with region("outs"):
-        outs = []
-        for i, (made, made_rows, out) in enumerate(
-            ((bk_ref, bk_rows, bk_out), (bv_ref, bv_rows, bv_out))
-        ):
-            by_head = jnp.stack([made[:, k * hd : (k + 1) * hd] for k in range(heads)], axis=0)
-            made_rows[...] = jnp.swapaxes(by_head, 0, 1)
-            outs.append(pltpu.make_async_copy(made_rows, out, out_sem.at[i]))
-            outs[-1].start()
+            snd_stats[k * per_head : (k + 1) * per_head] = packed
+        to_mergers(e_copy, 0, mergers)
+
+    def decode_values(k):
+        out = dacc[k]
+        for r in range(requests):
+            out += jnp.dot(
+                dlow[k, r], bv_ref[k, r * nb : (r + 1) * nb], preferred_element_type=f32
+            )
+        snd[k * per_head : (k + 1) * per_head] = out.reshape(per_head, share * pair, hd).astype(bf16)
+        to_mergers(d_copy, k * per_head, (k + 1) * per_head)
+
+    outs = []
+
+    def emit(made, made_rows, out):
+        made_rows[...] = jnp.swapaxes(made[...], 0, 1)
+        outs.append(pltpu.make_async_copy(made_rows, out, out_sem.at[len(outs)]))
+        outs[-1].start()
+
+    key_units = heads // 2
+    for i in range(len(units)):
+        with region(f"wwait{i}"):
+            w_wait(i)
+        product(i)
+        if i == len(units) - 2:
+            for j in range(key_units):
+                finish(j)
+            with region("decode"):
+                decode_weights()
+    for i in range(key_units, len(units)):
+        finish(i)
+        b, count = units[i]
+        with region("values"):
+            for at in range(b, b + count):
+                decode_values(at - heads)
+
+    emit(bk_ref, bk_rows, bk_out)
+    emit(bv_ref, bv_rows, bv_out)
 
     with region("drain"):
-        for c in range(CH):
-            for o in range(1, B):
-                p_copy(c, lax.rem(me + o, B), me).wait_send()
-        for kk in range(2):
-            for r in range(requests):
-                a_relay(kk, r).wait_send()
-        for v in range(2 * heads):
-            for x in range(2):
-
-                @pl.when((v // 2 % 2) * 2 + x != me)
-                def _(v=v, x=x):
-                    a_remote(jnp.int32(v), x).wait_send()
-
+        sent(psend.at[: B - 1], s_send)
+        sent(act.at[:2], p_send)
+        sent(stage.at[: requests * heads * (B - 1) // B], a_send)
         for way in range(2):
             for d in range(depth - 1):
                 shard, target, there = w_out(way, d)
 
                 @pl.when(there)
-                def _(way=way, d=d, shard=shard, target=target):
-                    for c in range(CH):
-                        w_copy(way, d, c, shard, target).wait_send()
-
-        @pl.when(me < B - 1)
+                def _(way=way, d=d, shard=shard):
+                    sent(wbuf.at[shard], w_send.at[way, d])
+
+        @pl.when((me < B - 1) | crosses)
         def _():
-            for p in range(2 * requests):
-                rim_near(p).wait_send()
-
-        @pl.when(crosses)
-        def _():
-            rim_near(0).wait_send()
-            for p in range(1, 2 * requests):
-                rim_far(p).wait_send()
+            sent(rimraw, rim_send)
 
         @pl.when(relays)
         def _():
-            rim_pass().wait_send()
-
-    with region("dwait"):
-        for o in range(1, n):
-            source = lax.rem(s + o, n)
-            e_copy(source, source).wait_recv()
-            d_copy(source, source).wait_recv()
-    landed = rcv[...].astype(f32)
-    attended = []
-    for j in range(share):
-        at = 2 * slots * j
-        peaks = rcv_stats[:, :, at : at + 1]
-        sums = rcv_stats[:, :, at + slots : at + slots + 1]
-        scale = jnp.exp(peaks - jnp.max(peaks, axis=0, keepdims=True))
-        mixed = jnp.sum(scale * landed[:, j * pair : (j + 1) * pair], axis=0)
-        attended.append(mixed / jnp.sum(scale * sums, axis=0))
-    att[s] = jnp.concatenate(attended, axis=0).astype(bf16)
-    for o in range(1, n):
-        t_copy(lax.rem(s + o, n), s).start()
+            sent(rimrel, rel_send)
+
+    def t_copy(to):
+        return remote(att.at[mine], att.at[mine], t_send, t_recv, to)
+
+    with region("merge"):
+
+        @pl.when(merges)
+        def _():
+            rcv[s] = snd[mine]
+            rcv_stats[s] = snd_stats[mine]
+            got(rcv_stats.at[: n - 1], e_recv)
+            got(rcv.at[: n - 1], d_recv)
+            landed = rcv[...].astype(f32)
+            attended = []
+            for j in range(share):
+                at = 2 * slots * j
+                peaks = rcv_stats[:, :, at : at + 1]
+                sums = rcv_stats[:, :, at + slots : at + slots + 1]
+                scale = jnp.exp(peaks - jnp.max(peaks, axis=0, keepdims=True))
+                mixed = jnp.sum(scale * landed[:, j * pair : (j + 1) * pair], axis=0)
+                attended.append(mixed / jnp.sum(scale * sums, axis=0))
+            att[mine] = jnp.concatenate(attended, axis=0).astype(bf16)
+            for o in range(1, n):
+                t_copy(lax.rem(s + o, n)).start()
+            sent(snd.at[: mergers - 1], d_send)
+            sent(snd_stats.at[: mergers - 1], e_send)
+
+        @pl.when(jnp.logical_not(merges))
+        def _():
+            sent(snd, d_send)
+            sent(snd_stats, e_send)
+
     ow_load.wait()
     with region("twait"):
-        for o in range(1, n):
-            d_copy(lax.rem(s + o, n), s).wait_send()
-            e_copy(lax.rem(s + o, n), s).wait_send()
-        for o in range(1, n):
-            source = lax.rem(s + o, n)
-            t_copy(source, source).wait_recv()
-    wide = [att[i].astype(f32) for i in range(n)]
+
+        @pl.when(merges)
+        def _():
+            got(att.at[: mergers - 1], t_recv)
+
+        @pl.when(jnp.logical_not(merges))
+        def _():
+            got(att, t_recv)
+
+    wide = [att[i].astype(f32) for i in range(mergers)]
     vectors = jnp.concatenate(
-        [wide[i][j * pair : (j + 1) * pair] for i in range(n) for j in range(share)], axis=1
+        [wide[i][j * pair : (j + 1) * pair] for i in range(mergers) for j in range(share)], axis=1
     ).astype(bf16)
     with region("outproj"):
-        partial_value = jnp.dot(vectors, owbuf[...], preferred_element_type=f32)
-        part[0] = partial_value
-    swap = remote(part.at[0], part.at[1], h_send, h_recv)
+        part[...] = jnp.dot(vectors, owbuf[...], preferred_element_type=f32)
+    swap = remote(part, part_out.at[h], h_send, h_recv)
     swap.start()
+    outs.append(pltpu.make_async_copy(part, part_out.at[h], out_sem.at[len(outs)]))
+    outs[-1].start()
     with region("swap"):
-        for o in range(1, n):
-            t_copy(lax.rem(s + o, n), s).wait_send()
-        swap.wait_recv()
-    first = jnp.where(h == 0, part[0], part[1])
-    second = jnp.where(h == 0, part[1], part[0])
-    summed = (first + second).astype(bf16)
-    for t in range(steps):
-        proj_rows[t] = summed[t * requests : (t + 1) * requests]
-    outs.append(pltpu.make_async_copy(proj_rows, proj_out, out_sem.at[2]))
-    outs[-1].start()
-    swap.wait_send()
-    with region("outwait"):
+
+        @pl.when(merges)
+        def _():
+            sent(rcv.at[: n - 1], t_send)
+
+        swap.wait()
         for copy in outs:
             copy.wait()
 
 
-def handed_on(keys_ref, values_ref, projected_ref, keys_out, values_out, projected_out):
+def handed_on(keys_ref, values_ref, part_ref, keys_out, values_out, projected_out):
     keys_out[...] = keys_ref[...]
     values_out[...] = values_ref[...]
-    projected_out[...] = projected_ref[...]
+    summed = (part_ref[0] + part_ref[1]).astype(projected_out.dtype)
+    steps, requests, _ = projected_out.shape
+    for t in range(steps):
+        projected_out[t] = summed[t * requests : (t + 1) * requests]
 
 
 def fused_body(
@@ -823,20 +838,22 @@
     rows = interval + OFF
     res = resident_keys.shape[1]
     feature, columns = beacon_wk.shape
-    width = 2 * columns // CH
+    blocks = 2 * columns // hd
+    units = blocks // 2 + 1
     pair = requests * steps
-    share = G * heads // n
+    mergers = min(2 * B, n)
+    share = G * heads // mergers
     bf16, f32 = jnp.bfloat16, jnp.float32
     dma = pltpu.SemaphoreType.DMA
     smem = pl.BlockSpec(memory_space=pltpu.SMEM)
     anywhere = pl.BlockSpec(memory_space=pl.ANY)
     vmem = pl.BlockSpec(memory_space=pltpu.VMEM)
-    keys, values, projected = pl.pallas_call(
+    keys, values, partial_sums = pl.pallas_call(
         functools.partial(fused_kernel, n),
         out_shape=(
             jax.ShapeDtypeStruct((requests * nb, heads, hd), bf16),
             jax.ShapeDtypeStruct((requests * nb, heads, hd), bf16),
-            jax.ShapeDtypeStruct((steps, requests, out_weight.shape[1]), bf16),
+            jax.ShapeDtypeStruct((2, pair, out_weight.shape[1]), f32),
         ),
         in_specs=[smem] * 3 + [anywhere] * 9,
         out_specs=(anywhere, anywhere, anywhere),
@@ -852,49 +869,51 @@
             pltpu.VMEM((requests, heads, rows, hd), bf16),
             pltpu.VMEM((requests, heads, rows, hd), bf16),
             pltpu.VMEM((G, nb, hd), bf16),
-            pltpu.VMEM((depth, CH, feature, width), bf16),
+            pltpu.VMEM((depth, blocks, feature, hd), bf16),
             pltpu.VMEM((depth, requests, B, nb, feature), bf16),
             pltpu.VMEM((requests * heads, 2, nb, feature), bf16),
-            pltpu.VMEM((B, CH, requests * nb, width), bf16),
-            pltpu.VMEM((B, CH, requests * nb, width), bf16),
-            pltpu.VMEM((CH, requests * nb, width), f32),
+            pltpu.VMEM((B, blocks, requests * nb, hd), bf16),
+            pltpu.VMEM((B, blocks, requests * nb, hd), bf16),
+            pltpu.VMEM((blocks, requests * nb, hd), f32),
             pltpu.VMEM((requests, nb, rows), f32),
             pltpu.VMEM(out_weight.shape, bf16),
             pltpu.VMEM((requests, heads, res, hd), bf16),
             pltpu.VMEM((requests, heads, res, hd), bf16),
             pltpu.VMEM((heads, G * pair, hd), bf16),
-            pltpu.VMEM((requests * nb, columns), bf16),
-            pltpu.VMEM((requests * nb, columns), bf16),
+            pltpu.VMEM((heads, requests * nb, hd), bf16),
+            pltpu.VMEM((heads, requests * nb, hd), bf16),
+            pltpu.VMEM((heads, G * pair, hd), f32),
+            pltpu.VMEM((heads, requests, G * pair, nb), bf16),
+            pltpu.VMEM((mergers, share * pair, hd), bf16),
+            pltpu.VMEM((mergers, pair, hd), f32),
             pltpu.VMEM((n, share * pair, hd), bf16),
             pltpu.VMEM((n, pair, hd), f32),
-            pltpu.VMEM((n, share * pair, hd), bf16),
-            pltpu.VMEM((n, pair, hd), f32),
-            pltpu.VMEM((n, share * pair, hd), bf16),
-            pltpu.VMEM((2, pair, out_weight.shape[1]), f32),
+            pltpu.VMEM((mergers, share * pair, hd), bf16),
+            pltpu.VMEM((pair, out_weight.shape[1]), f32),
             pltpu.VMEM((requests * nb, heads, hd), bf16),
             pltpu.VMEM((requests * nb, heads, hd), bf16),
-            pltpu.VMEM((steps, requests, out_weight.shape[1]), bf16),
-            dma((CH + 2 * requests + 5,)),
+            dma((2 * requests + 5,)),
+            dma((units,)),
             dma((3,)),
-            dma((2 * requests,)),
-            dma((2 * requests,)),
-            dma,
-            dma,
-            dma((2, depth - 1, CH)),
-            dma((2, depth - 1, CH)),
-            dma((requests * heads, 2)),
-            dma((2, requests, B)),
+            dma,
+            dma((requests,)),
+            dma,
+            dma,
+            dma((2, depth - 1)),
+            dma((2, depth - 1, units)),
+            dma,
             dma((2, requests)),
             dma((2, requests)),
-            dma((2, requests)),
-            dma((B, CH)),
-            dma((B, CH)),
-            dma((n,)),
-            dma((n,)),
-            dma((n,)),
-            dma((n,)),
-            dma((n,)),
-            dma((n,)),
+            dma,
+            dma,
+            dma,
+            dma((units,)),
+            dma,
+            dma,
+            dma,
+            dma,
+            dma,
+            dma,
             dma,
             dma,
         ],
@@ -917,10 +936,14 @@
     )
     keys, values, projected = pl.pallas_call(
         handed_on,
-        out_shape=tuple(jax.ShapeDtypeStruct(x.shape, x.dtype) for x in (keys, values, projected)),
+        out_shape=(
+            jax.ShapeDtypeStruct(keys.shape, bf16),
+            jax.ShapeDtypeStruct(values.shape, bf16),
+            jax.ShapeDtypeStruct((steps, requests, out_weight.shape[1]), bf16),
+        ),
         in_specs=[vmem] * 3,
         out_specs=(vmem,) * 3,
-    )(keys, values, projected)
+    )(keys, values, partial_sums)
     return (
         keys.reshape(requests, nb, heads, hd),
         values.reshape(requests, nb, heads, hd),

time: 111 us -> 103 us (0.928)
  Pallas kernels: 110 us -> 102 us
    pallas_call x1, Pallas kernels: 108 us -> 100 us  [fused_body(): pl.pallas_call(functools.partial(fused_kernel, n), out_shape=(jax.ShapeDt...]
where the time goes in v3:
time: 103 us
  Pallas kernels  102 us (99%)
    pallas_call x1, Pallas kernels, fused_body(): pl.pallas_call(functools.partial(fused_kernel, n), out_shape=(jax.ShapeDt...  100 us

profile of v3, /device:TPU:0, one launch (start us, length us, event | category | flops | bytes accessed | tf_op | source)
XLA Modules:
  0.0 102.9 jit_solution(14829451654723536291)
XLA Ops:
  0.6 100.4 %shard_map.139 = (bf16[256,4,128]{2,1,0:T(4,128)(2,1)}, bf16[256,4,128]{2,1,0:T(4,128)(2,1)}, f32[2,8,512]{2,1,0:T(8,128)}) custom-call(s32[2]{0:T(128)} %phase_ref.1, s32[2,16]{1,0:T(2,128)} %ratio_ref.1, s32[2,16]{1,0:T(2,128)} %rlen_ref.1, bf16[2,1024,4,128]{3,2,1,0:T(4,128)(2,1)} %k_hbm.1, bf16[2,1024,4,128]{3,2,1,0:T(4,128)(2,1)} %v_hbm.1, ...), custom_call_target="tpu_custom_call" | custom-call | tf_op jit(solution)/shard_map/pallas_call | solution.py:851
  101.1 1.8 %shard_map.140 = (bf16[256,4,128]{2,1,0:T(4,128)(2,1)}, bf16[256,4,128]{2,1,0:T(4,128)(2,1)}, bf16[4,2,512]{2,1,0:T(2,128)(2,1)}) custom-call(bf16[256,4,128]{2,1,0:T(4,128)(2,1)} %get-tuple-element.9.keys_ref, bf16[256,4,128]{2,1,0:T(4,128)(2,1)} %get-tuple-element.10.values_ref, f32[2,8,512]{2,1,0:T(8,128)} %get-tuple-element.11.part_ref), custom_call_target="tpu_custom_call" | custom-call | tf_op jit(solution)/shard_map/pallas_call | solution.py:937

commit v4 on v3

--- a/solution.py
+++ b/solution.py
@@ -171,6 +171,8 @@
 
 
 B = 4
+GB = 2
+STRAIGHT = 2
 
 
 def fused_kernel(
@@ -206,7 +208,10 @@
     stage,
     psend,
     precv,
+    pdiag,
+    hold,
     own,
+    acc,
     bias,
     owbuf,
     rk_ref,
@@ -215,6 +220,7 @@
     bk_ref,
     bv_ref,
     dacc,
+    dstat,
     dlow,
     snd,
     snd_stats,
@@ -240,6 +246,7 @@
     p_recv,
     s_send,
     s_recv,
+    g_recv,
     d_send,
     d_recv,
     e_send,
@@ -257,10 +264,11 @@
     me = lax.rem(s, B)
     requests, interval, heads, hd = kraw.shape
     rows = interval + OFF
-    nb = bias.shape[1]
+    nb = psend.shape[2] // requests
     blocks = wbuf.shape[1]
     units = [(b, 2) for b in range(0, blocks - 2, 2)] + [(blocks - 2, 1), (blocks - 1, 1)]
     inv_root = 1.0 / math.sqrt(hd)
+    to_log2 = inv_root / math.log(2.0)
     f32 = jnp.float32
     bf16 = jnp.bfloat16
 
@@ -280,6 +288,18 @@
 
     def sent(ref, sem):
         remote(ref, ref, sem, sem, s).wait_send()
+
+    barrier = pltpu.get_barrier_semaphore()
+    for o in range(1, n):
+        pl.semaphore_signal(
+            barrier,
+            inc=1,
+            device_id={"seq": lax.rem(s + o, n)},
+            device_id_type=pl.DeviceIdType.MESH,
+        )
+    pl.semaphore_signal(
+        barrier, inc=1, device_id={"head": 1 - h}, device_id_type=pl.DeviceIdType.MESH
+    )
 
     loads = []
 
@@ -301,17 +321,6 @@
     ow_load = load(ow_hbm, owbuf)
 
     with region("barrier"):
-        barrier = pltpu.get_barrier_semaphore()
-        for o in range(1, n):
-            pl.semaphore_signal(
-                barrier,
-                inc=1,
-                device_id={"seq": lax.rem(s + o, n)},
-                device_id_type=pl.DeviceIdType.MESH,
-            )
-        pl.semaphore_signal(
-            barrier, inc=1, device_id={"head": 1 - h}, device_id_type=pl.DeviceIdType.MESH
-        )
         pl.semaphore_wait(barrier, n)
 
     crosses = (me == B - 1) & (z < depth - 1)
@@ -337,8 +346,7 @@
     @pl.when(crosses)
     def _():
         rim_near(0).start()
-        for p in range(1, 2 * requests):
-            rim_far(p).start()
+        rim_far(1).start()
 
     def w_copy(way, d, i, shard, target):
         b, count = units[i]
@@ -382,12 +390,14 @@
                 w_copy(way, d - 1, i, shard, z).wait_recv()
                 w_copy(way, d, i, shard, target).start()
 
-    def w_wait(i):
+    ends = (z == 0) | (z == depth - 1)
+    far = depth - 1 - z
+
+    def w_wait(i, first, end):
         for way in range(2):
-            for d in range(depth - 1):
+            for d in range(first, end):
                 shard, there = w_in(way, d)
-                if d < depth - 2:
-                    there = there & ((z == depth - 1) if way == 0 else (z == 0))
+                there = there & ((z == depth - 1) if way == 0 else (z == 0))
 
                 @pl.when(there)
                 def _(way=way, d=d, shard=shard):
@@ -402,23 +412,24 @@
 
     @pl.when(me != 1)
     def _():
-        w_own(1, 2)
-
-    @pl.when((me == 0) | (me == B - 1))
-    def _():
-        w_own(2, len(units))
+        w_own(1, len(units))
 
     with region("prep"):
         for r in range(requests):
-            slot = lax.broadcasted_iota(jnp.int32, (nb, rows), 0)
-            position = lax.broadcasted_iota(jnp.int32, (nb, rows), 1) - OFF + phase_ref[r]
+            slot = lax.broadcasted_iota(jnp.int32, (rows, nb), 1)
+            position = lax.broadcasted_iota(jnp.int32, (rows, nb), 0) - OFF + phase_ref[r]
             lead = jnp.where(s == 0, phase_ref[r], 0)
             reach = (slot + 1) * ratio_ref[r, s] + lead
             allowed = (position >= lead) & (position < interval) & (position < reach)
-            bias[r] = jnp.where(allowed, 0.0, masked_score).astype(f32)
+            bias[r] = jnp.where(allowed, 0.0, masked_score).astype(bf16)
         for p in range(2 * requests):
             kv_load[p].wait()
             (kbuf, vbuf)[p % 2][p // 2, :, OFF:] = jnp.swapaxes((kraw, vraw)[p % 2][p // 2], 0, 1)
+        chosen = lax.broadcasted_iota(jnp.int32, (nb, nb), 0) == lax.broadcasted_iota(
+            jnp.int32, (nb, nb), 1
+        )
+        for g in range(G):
+            qbuf[g, :, hd:] = jnp.where(chosen, 1.0, 0.0).astype(bf16)
         for copy in rest_load:
             copy.wait()
         for r in range(requests):
@@ -433,17 +444,18 @@
             dq_ref[k] = jnp.swapaxes(asked, 0, 1).reshape(G * pair, hd).astype(bf16)
         q_load.wait()
 
-    @pl.when(relays & (me != 0))
+    @pl.when(relays & (me == 1))
     def _():
         rim_relay()
 
+    @pl.when(crosses)
+    def _():
+        for p in range(2, 2 * requests):
+            rim_far(p).start()
+
     @pl.when(me == 1)
     def _():
-        w_own(1, 2)
-
-    @pl.when((me == 1) | (me == 2))
-    def _():
-        w_own(2, len(units))
+        w_own(1, len(units))
 
     @pl.when(s == 0)
     def _():
@@ -487,23 +499,26 @@
             vbuf[r, :, :OFF] = jnp.swapaxes(rimraw[r * 2 + 1], 0, 1)
 
         with region("att"):
-            qbuf[...] = jnp.swapaxes(qraw[r, :, k], 0, 1)
-            for g in range(G):
-                scores = (
-                    lax.dot_general(
-                        qbuf[g],
-                        kbuf[r, k],
-                        (((1,), (1,)), ((), ())),
-                        preferred_element_type=f32,
-                    )
-                    * inv_root
-                    + bias[r]
+            qbuf[:, :, :hd] = jnp.swapaxes(qraw[r, :, k], 0, 1)
+            ones = jnp.ones((rows, hd), bf16)
+            for first in range(0, G, GB):
+                scores = lax.dot_general(
+                    qbuf[first : first + GB].reshape(GB * nb, hd + nb),
+                    jnp.concatenate([kbuf[r, k], bias[r]], axis=1),
+                    (((1,), (1,)), ((), ())),
+                    preferred_element_type=f32,
                 )
-                weights = jnp.exp(scores - jnp.max(scores, axis=-1, keepdims=True))
-                total = jnp.sum(weights, axis=-1, keepdims=True)
-                out = jnp.dot(weights.astype(bf16), vbuf[r, k], preferred_element_type=f32)
-                at = (g % 4) * hd
-                stage[v, g // 4, :, at : at + hd] = (out / total).astype(bf16)
+                peak = jnp.max(scores, axis=-1, keepdims=True)
+                weights = jnp.exp2((scores - peak) * to_log2).astype(bf16)
+                out = jnp.dot(
+                    weights,
+                    jnp.concatenate([vbuf[r, k], ones], axis=1),
+                    preferred_element_type=f32,
+                )
+                out = (out[:, :hd] / out[:, hd:]).astype(bf16)
+                for g in range(first, first + GB):
+                    at = (g % 4) * hd
+                    stage[v, g // 4, :, at : at + hd] = out[(g - first) * nb : (g - first + 1) * nb]
         for x in range(2):
             member = lax.rem(k, 2) * 2 + x
 
@@ -517,21 +532,15 @@
 
         with region("relay"):
 
+            @pl.when((u == jnp.where(me == 0, 1, 0)) & (me != 1) & relays)
+            def _():
+                rim_relay()
+
             for i in range(len(units)):
 
-                @pl.when(u == min(i, heads - 1))
+                @pl.when(u == min(i + 1 + i // 2, heads + 1))
                 def _(i=i):
                     w_relay(1, i)
-
-            @pl.when((u == 0) & (me == 0) & relays)
-            def _():
-                rim_relay()
-
-            for i in range(len(units) - 2):
-
-                @pl.when(u == heads + 1 + i)
-                def _(i=i):
-                    w_relay(2, i)
 
             @pl.when(u == heads + 1)
             def _():
@@ -540,21 +549,45 @@
             @pl.when(u == heads + 3)
             def _():
                 a_gather(1, 0)
+                w_relay(2, 0)
 
         return carry
 
     lax.fori_loop(0, 2 * heads, unit, 0)
     with region("gather"):
         a_gather(0, 1)
-        w_relay(2, len(units) - 2)
-        w_relay(2, len(units) - 1)
         a_gather(1, 1)
+        for i in range(1, len(units)):
+            w_relay(2, i)
         got(act.at[:2], p_recv)
 
-    def p_copy(i, to, frm):
-        b, count = units[i]
+    x_side = me + 1 - 2 * lax.rem(me, 2)
+    y_side = lax.rem(me + 2, B)
+    across = B - 1 - me
+    straight = blocks - STRAIGHT
+
+    def p_copy(lane, at):
+        if at >= straight:
+            i = min(at // 2, len(units) - 2) + (at == blocks - 1)
+            return remote(
+                psend.at[lane, at],
+                pdiag.at[at] if lane == 0 else precv.at[lane - 1, at],
+                s_send,
+                (g_recv if lane == 0 else s_recv).at[i],
+                z * B + (across, x_side, y_side)[lane],
+            )
+        if lane == 0:
+            side, target = at % 2, pdiag.at[at]
+        else:
+            side = at % 2 if lane == 1 else 1 - at % 2
+            target = precv.at[side, at]
+        i = min(at // 2, len(units) - 2) + (at == blocks - 1)
         return remote(
-            psend.at[to, b : b + count], precv.at[frm, b : b + count], s_send, s_recv.at[i], z * B + to
+            psend.at[lane, at],
+            target,
+            s_send,
+            (g_recv if lane == 0 else s_recv).at[i],
+            z * B + (x_side, y_side)[side],
         )
 
     slot_row = lax.broadcasted_iota(jnp.int32, (nb, hd), 0)
@@ -562,11 +595,15 @@
     def finish(i):
         b, count = units[i]
         with region(f"finish{i}"):
-            got(precv.at[: B - 1, b : b + count], s_recv.at[i])
+            got(precv.at[:, b : b + count], s_recv.at[i])
+            if b >= straight:
+                got(pdiag.at[b : b + count], g_recv.at[i])
         for at in range(b, b + count):
             total = own[at]
-            for o in range(1, B):
-                total += precv[lax.rem(me + o, B), at].astype(f32)
+            for side in range(2):
+                total += precv[side, at].astype(f32)
+            if b >= straight:
+                total += pdiag[at].astype(f32)
             out_ref = (bk_ref, bv_ref)[at // heads]
             for r in range(requests):
                 live = (slot_row + 1) * ratio_ref[r, s] <= interval
@@ -574,38 +611,88 @@
                     live, total[r * nb : (r + 1) * nb], 0.0
                 ).astype(bf16)
 
-    def product(i):
+    def times(zi, to, b, count):
+        return jnp.dot(
+            act[zi, :, to].reshape(requests * nb, act.shape[4]),
+            jnp.concatenate([wbuf[zi, at] for at in range(b, b + count)], axis=1),
+            preferred_element_type=f32,
+        )
+
+    def near_products():
+        near = jnp.where(z == 0, 0, 1)
+        for b in range(0, blocks, 2):
+            for i in range(len(units)):
+                if b <= units[i][0] < b + 2:
+                    w_wait(i, 0, depth - 2)
+
+            def step(to, carry, b=b):
+                total = times(near, to, b, 2)
+                for zi in range(1, depth - 1):
+                    total += times(near + zi, to, b, 2)
+                for at in range(2):
+                    acc[to, b + at] = total[:, at * hd : (at + 1) * hd]
+                return carry
+
+            lax.fori_loop(0, B, step, 0)
+
+    def product(i, late):
         b, count = units[i]
 
         def step(o, carry):
-            to = lax.rem(me + 1 + o, B)
-            total = jnp.zeros((requests * nb, count * hd), f32)
-            for zi in range(depth):
-                total += jnp.dot(
-                    act[zi, :, to].reshape(requests * nb, act.shape[4]),
-                    jnp.concatenate([wbuf[zi, at] for at in range(b, b + count)], axis=1),
-                    preferred_element_type=f32,
-                )
-
-            @pl.when(o < B - 1)
+            to = jnp.where(o == 0, across, jnp.where(o == 1, x_side, jnp.where(o == 2, y_side, me)))
+            if late:
+                total = jnp.concatenate([acc[to, b + at] for at in range(count)], axis=1)
+                total += times(far, to, b, count)
+            else:
+                total = times(0, to, b, count)
+                for zi in range(1, depth):
+                    total += times(zi, to, b, count)
+
+            def part_of(at):
+                return total[:, (at - b) * hd : (at - b + 1) * hd]
+
+            @pl.when(o == 0)
             def _():
-                for at in range(count):
-                    psend[to, b + at] = total[:, at * hd : (at + 1) * hd].astype(bf16)
-                p_copy(i, to, me).start()
+                for at in range(b, b + count):
+                    psend[0, at] = part_of(at).astype(bf16)
+                    p_copy(0, at).start()
+
+            for side in range(2):
+
+                @pl.when(o == 1 + side)
+                def _(side=side):
+                    for at in range(b, b + count):
+                        if at >= straight:
+                            psend[1 + side, at] = part_of(at).astype(bf16)
+                            p_copy(1 + side, at).start()
+                        elif at % 2 == side:
+                            psend[1, at] = part_of(at).astype(bf16)
+                            p_copy(1, at).start()
+                        else:
+                            hold[at] = part_of(at)
 
             @pl.when(o == B - 1)
             def _():
-                for at in range(count):
-                    own[b + at] = total[:, at * hd : (at + 1) * hd]
+                for at in range(b, b + count):
+                    own[at] = part_of(at)
 
             return carry
 
         with region(f"prod{i}"):
             lax.fori_loop(0, B, step, 0)
 
+    def forward(i):
+        b, count = units[i]
+        if b >= straight:
+            return
+        with region(f"forward{i}"):
+            got(pdiag.at[b : b + count], g_recv.at[i])
+            for at in range(b, b + count):
+                psend[2, at] = (hold[at] + pdiag[at].astype(f32)).astype(bf16)
+                p_copy(2, at).start()
+
     res = rk_ref.shape[2]
     qrows = dq_ref.shape[1]
-    cells = res + nb + OFF
     mergers = snd.shape[0]
     share = G * heads // mergers
     slots = hd // (2 * share)
@@ -627,56 +714,61 @@
             def _(to=to):
                 copy(to).start()
 
-    def decode_weights():
-        row_request = lax.rem(lax.broadcasted_iota(jnp.int32, (qrows, cells), 0), requests)
-        cell = lax.broadcasted_iota(jnp.int32, (qrows, cells), 1)
+    def scored(k, r, key, mask):
+        scores = lax.dot_general(
+            dq_ref[k], key, (((1,), (1,)), ((), ())), preferred_element_type=f32
+        )
+        return jnp.where(mask, scores * inv_root, masked_score)
+
+    def row_of(count):
+        return (
+            lax.rem(lax.broadcasted_iota(jnp.int32, (qrows, count), 0), requests),
+            lax.broadcasted_iota(jnp.int32, (qrows, count), 1),
+        )
+
+    def decode_early():
+        row_request, cell = row_of(res)
+        row_rim, rim = row_of(OFF)
         last = jnp.where(s == n - 1, 1, 0)
-        masks = []
-        for r in range(requests):
-            usable = (
-                (cell < rlen_ref[r, s])
-                | (
-                    (cell >= res)
-                    & (cell < res + nb)
-                    & ((cell - res + 1) * ratio_ref[r, s] <= interval)
-                )
-                | ((cell >= res + nb + OFF - phase_ref[r] * last) & (cell >= res + nb))
-            )
-            masks.append(usable & (row_request == r))
         for k in range(heads):
             pieces = []
             for r in range(requests):
-                keys = (
-                    rk_ref[r, k],
-                    bk_ref[k, r * nb : (r + 1) * nb],
-                    kbuf[r, k, rows - OFF :],
-                )
-                scores = jnp.concatenate(
-                    [
-                        lax.dot_general(
-                            dq_ref[k], key, (((1,), (1,)), ((), ())), preferred_element_type=f32
-                        )
-                        for key in keys
-                    ],
-                    axis=1,
-                )
-                pieces.append(jnp.where(masks[r], scores * inv_root, masked_score))
-            peak = jnp.maximum(
-                jnp.max(pieces[0], axis=-1, keepdims=True),
-                jnp.max(pieces[1], axis=-1, keepdims=True),
-            )
+                usable = (cell < rlen_ref[r, s]) & (row_request == r)
+                pieces.append((scored(k, r, rk_ref[r, k], usable), rv_ref, r, slice(0, res)))
+                usable = (rim >= OFF - phase_ref[r] * last) & (row_rim == r)
+                left = slice(rows - OFF, rows)
+                pieces.append((scored(k, r, kbuf[r, k, left], usable), vbuf, r, left))
+            peak = jnp.max(pieces[0][0], axis=-1, keepdims=True)
+            for piece in pieces[1:]:
+                peak = jnp.maximum(peak, jnp.max(piece[0], axis=-1, keepdims=True))
             total = jnp.zeros((qrows, 1), f32)
             out = jnp.zeros((qrows, hd), f32)
+            for scores, source, r, span in pieces:
+                weights = jnp.exp(scores - peak)
+                total += jnp.sum(weights, axis=-1, keepdims=True)
+                out += jnp.dot(weights.astype(bf16), source[r, k, span], preferred_element_type=f32)
+            dacc[k] = out
+            dstat[k, 0] = jnp.broadcast_to(peak, (qrows, hd))
+            dstat[k, 1] = jnp.broadcast_to(total, (qrows, hd))
+
+    def decode_weights():
+        row_request, slot = row_of(nb)
+        for k in range(heads):
+            pieces = []
+            for r in range(requests):
+                usable = ((slot + 1) * ratio_ref[r, s] <= interval) & (row_request == r)
+                pieces.append(scored(k, r, bk_ref[k, r * nb : (r + 1) * nb], usable))
+            former = dstat[k, 0]
+            peak = former
+            for piece in pieces:
+                peak = jnp.maximum(peak, jnp.max(piece, axis=-1, keepdims=True))
+            scale = jnp.exp(former - peak)
+            total = dstat[k, 1] * scale
             for r in range(requests):
                 weights = jnp.exp(pieces[r] - peak)
                 total += jnp.sum(weights, axis=-1, keepdims=True)
-                low = weights.astype(bf16)
-                dlow[k, r] = low[:, res : res + nb]
-                out += jnp.dot(low[:, :res], rv_ref[r, k], preferred_element_type=f32)
-                out += jnp.dot(
-                    low[:, res + nb :], vbuf[r, k, rows - OFF :], preferred_element_type=f32
-                )
-            dacc[k] = out
+                dlow[k, r] = weights.astype(bf16)
+            dacc[k] = dacc[k] * scale
             lane = lax.broadcasted_iota(jnp.int32, (qrows, hd), 1)
             stats = jnp.where(lax.rem(lane // slots, 2) == 0, peak, total)
             stats = stats.reshape(per_head, share, pair, hd)
@@ -704,15 +796,33 @@
         outs[-1].start()
 
     key_units = heads // 2
+
+    @pl.when(ends)
+    def _():
+        with region("near"):
+            near_products()
+
     for i in range(len(units)):
-        with region(f"wwait{i}"):
-            w_wait(i)
-        product(i)
-        if i == len(units) - 2:
-            for j in range(key_units):
-                finish(j)
-            with region("decode"):
-                decode_weights()
+        @pl.when(ends)
+        def _(i=i):
+            with region(f"wwait{i}"):
+                w_wait(i, depth - 2, depth - 1)
+            product(i, True)
+
+        @pl.when(jnp.logical_not(ends))
+        def _(i=i):
+            product(i, False)
+
+        if i > 0:
+            forward(i - 1)
+        if i == 1:
+            with region("early"):
+                decode_early()
+    forward(len(units) - 1)
+    for i in range(key_units):
+        finish(i)
+    with region("decode"):
+        decode_weights()
     for i in range(key_units, len(units)):
         finish(i)
         b, count = units[i]
@@ -724,7 +834,7 @@
     emit(bv_ref, bv_rows, bv_out)
 
     with region("drain"):
-        sent(psend.at[: B - 1], s_send)
+        sent(psend, s_send)
         sent(act.at[:2], p_send)
         sent(stage.at[: requests * heads * (B - 1) // B], a_send)
         for way in range(2):
@@ -743,8 +853,11 @@
         def _():
             sent(rimrel, rel_send)
 
+    early = mergers - mergers // heads
+    late = jnp.where(mine >= early, 1, 0)
+
     def t_copy(to):
-        return remote(att.at[mine], att.at[mine], t_send, t_recv, to)
+        return remote(att.at[mine], att.at[mine], t_send, t_recv.at[late], to)
 
     with region("merge"):
 
@@ -775,22 +888,28 @@
             sent(snd_stats, e_send)
 
     ow_load.wait()
+
+    def attended_rows(first, end, group):
+        @pl.when(merges & (late == group))
+        def _():
+            got(att.at[first : end - 1], t_recv.at[group])
+
+        @pl.when(jnp.logical_not(merges & (late == group)))
+        def _():
+            got(att.at[first:end], t_recv.at[group])
+
+        wide = [att[i].astype(f32) for i in range(first, end)]
+        vectors = jnp.concatenate(
+            [piece[j * pair : (j + 1) * pair] for piece in wide for j in range(share)], axis=1
+        ).astype(bf16)
+        span = share * hd
+        return jnp.dot(vectors, owbuf[first * span : end * span], preferred_element_type=f32)
+
     with region("twait"):
-
-        @pl.when(merges)
-        def _():
-            got(att.at[: mergers - 1], t_recv)
-
-        @pl.when(jnp.logical_not(merges))
-        def _():
-            got(att, t_recv)
-
-    wide = [att[i].astype(f32) for i in range(mergers)]
-    vectors = jnp.concatenate(
-        [wide[i][j * pair : (j + 1) * pair] for i in range(mergers) for j in range(share)], axis=1
-    ).astype(bf16)
-    with region("outproj"):
-        part[...] = jnp.dot(vectors, owbuf[...], preferred_element_type=f32)
+        sums = attended_rows(0, early, 0)
+    with region("twait2"):
+        sums += attended_rows(early, mergers, 1)
+    part[...] = sums
     swap = remote(part, part_out.at[h], h_send, h_recv)
     swap.start()
     outs.append(pltpu.make_async_copy(part, part_out.at[h], out_sem.at[len(outs)]))
@@ -868,14 +987,17 @@
             pltpu.VMEM((OFF, heads, hd), bf16),
             pltpu.VMEM((requests, heads, rows, hd), bf16),
             pltpu.VMEM((requests, heads, rows, hd), bf16),
-            pltpu.VMEM((G, nb, hd), bf16),
+            pltpu.VMEM((G, nb, hd + nb), bf16),
             pltpu.VMEM((depth, blocks, feature, hd), bf16),
             pltpu.VMEM((depth, requests, B, nb, feature), bf16),
             pltpu.VMEM((requests * heads, 2, nb, feature), bf16),
-            pltpu.VMEM((B, blocks, requests * nb, hd), bf16),
-            pltpu.VMEM((B, blocks, requests * nb, hd), bf16),
+            pltpu.VMEM((3, blocks, requests * nb, hd), bf16),
+            pltpu.VMEM((2, blocks, requests * nb, hd), bf16),
+            pltpu.VMEM((blocks, requests * nb, hd), bf16),
             pltpu.VMEM((blocks, requests * nb, hd), f32),
-            pltpu.VMEM((requests, nb, rows), f32),
+            pltpu.VMEM((blocks, requests * nb, hd), f32),
+            pltpu.VMEM((B, blocks, requests * nb, hd), f32),
+            pltpu.VMEM((requests, rows, nb), bf16),
             pltpu.VMEM(out_weight.shape, bf16),
             pltpu.VMEM((requests, heads, res, hd), bf16),
             pltpu.VMEM((requests, heads, res, hd), bf16),
@@ -883,6 +1005,7 @@
             pltpu.VMEM((heads, requests * nb, hd), bf16),
             pltpu.VMEM((heads, requests * nb, hd), bf16),
             pltpu.VMEM((heads, G * pair, hd), f32),
+            pltpu.VMEM((heads, 2, G * pair, hd), f32),
             pltpu.VMEM((heads, requests, G * pair, nb), bf16),
             pltpu.VMEM((mergers, share * pair, hd), bf16),
             pltpu.VMEM((mergers, pair, hd), f32),
@@ -908,12 +1031,13 @@
             dma,
             dma,
             dma((units,)),
-            dma,
-            dma,
-            dma,
-            dma,
-            dma,
-            dma,
+            dma((units,)),
+            dma,
+            dma,
+            dma,
+            dma,
+            dma,
+            dma((2,)),
             dma,
             dma,
         ],

time: 103 us -> 102 us (level)
  no operation moved by 1% of the time
where the time goes in v4:
time: 102 us
  Pallas kernels  101 us (99%)
    pallas_call x1, Pallas kernels, fused_body(): pl.pallas_call(functools.partial(fused_kernel, n), out_shape=(jax.ShapeDt...  99.6 us

profile of v4, /device:TPU:0, one launch (start us, length us, event | category | flops | bytes accessed | tf_op | source)
XLA Modules:
  0.0 102.1 jit_solution(9067696398495847620)
XLA Ops:
  0.6 99.6 %shard_map.139 = (bf16[256,4,128]{2,1,0:T(4,128)(2,1)}, bf16[256,4,128]{2,1,0:T(4,128)(2,1)}, f32[2,8,512]{2,1,0:T(8,128)}) custom-call(s32[2]{0:T(128)} %phase_ref.1, s32[2,16]{1,0:T(2,128)} %ratio_ref.1, s32[2,16]{1,0:T(2,128)} %rlen_ref.1, bf16[2,1024,4,128]{3,2,1,0:T(4,128)(2,1)} %k_hbm.1, bf16[2,1024,4,128]{3,2,1,0:T(4,128)(2,1)} %v_hbm.1, ...), custom_call_target="tpu_custom_call" | custom-call | tf_op jit(solution)/shard_map/pallas_call | solution.py:970
  100.2 1.8 %shard_map.140 = (bf16[256,4,128]{2,1,0:T(4,128)(2,1)}, bf16[256,4,128]{2,1,0:T(4,128)(2,1)}, bf16[4,2,512]{2,1,0:T(2,128)(2,1)}) custom-call(bf16[256,4,128]{2,1,0:T(4,128)(2,1)} %get-tuple-element.9.keys_ref, bf16[256,4,128]{2,1,0:T(4,128)(2,1)} %get-tuple-element.10.values_ref, f32[2,8,512]{2,1,0:T(8,128)} %get-tuple-element.11.part_ref), custom_call_target="tpu_custom_call" | custom-call | tf_op jit(solution)/shard_map/pallas_call | solution.py:1061

commit v5 on v4

--- a/solution.py
+++ b/solution.py
@@ -536,11 +536,15 @@
             def _():
                 rim_relay()
 
-            for i in range(len(units)):
-
-                @pl.when(u == min(i + 1 + i // 2, heads + 1))
+            for i in range(3):
+
+                @pl.when(u == heads - 2 + i)
                 def _(i=i):
                     w_relay(1, i)
+
+            @pl.when(u == heads + 2)
+            def _():
+                w_relay(2, 0)
 
             @pl.when(u == heads + 1)
             def _():
@@ -549,16 +553,17 @@
             @pl.when(u == heads + 3)
             def _():
                 a_gather(1, 0)
-                w_relay(2, 0)
 
         return carry
 
     lax.fori_loop(0, 2 * heads, unit, 0)
     with region("gather"):
+        w_relay(2, 1)
         a_gather(0, 1)
         a_gather(1, 1)
-        for i in range(1, len(units)):
-            w_relay(2, i)
+        w_relay(2, 2)
+        w_relay(1, 3)
+        w_relay(1, 4)
         got(act.at[:2], p_recv)
 
     x_side = me + 1 - 2 * lax.rem(me, 2)
@@ -590,6 +595,7 @@
             z * B + (x_side, y_side)[side],
         )
 
+    key_units = heads // 2
     slot_row = lax.broadcasted_iota(jnp.int32, (nb, hd), 0)
 
     def finish(i):
@@ -618,22 +624,24 @@
             preferred_element_type=f32,
         )
 
+    ahead = units[key_units + 1][0]
+
     def near_products():
         near = jnp.where(z == 0, 0, 1)
-        for b in range(0, blocks, 2):
-            for i in range(len(units)):
-                if b <= units[i][0] < b + 2:
-                    w_wait(i, 0, depth - 2)
+        for i in range(key_units + 1, len(units)):
+            w_wait(i, 0, depth - 2)
+        for b in range(ahead, blocks, 2):
 
             def step(to, carry, b=b):
                 total = times(near, to, b, 2)
                 for zi in range(1, depth - 1):
                     total += times(near + zi, to, b, 2)
                 for at in range(2):
-                    acc[to, b + at] = total[:, at * hd : (at + 1) * hd]
+                    acc[to, b - ahead + at] = total[:, at * hd : (at + 1) * hd]
                 return carry
 
-            lax.fori_loop(0, B, step, 0)
+            with region("near"):
+                lax.fori_loop(0, B, step, 0)
 
     def product(i, late):
         b, count = units[i]
@@ -641,7 +649,7 @@
         def step(o, carry):
             to = jnp.where(o == 0, across, jnp.where(o == 1, x_side, jnp.where(o == 2, y_side, me)))
             if late:
-                total = jnp.concatenate([acc[to, b + at] for at in range(count)], axis=1)
+                total = jnp.concatenate([acc[to, b - ahead + at] for at in range(count)], axis=1)
                 total += times(far, to, b, count)
             else:
                 total = times(0, to, b, count)
@@ -795,26 +803,30 @@
         outs.append(pltpu.make_async_copy(made_rows, out, out_sem.at[len(outs)]))
         outs[-1].start()
 
-    key_units = heads // 2
-
-    @pl.when(ends)
-    def _():
-        with region("near"):
-            near_products()
-
     for i in range(len(units)):
+
         @pl.when(ends)
         def _(i=i):
+            late = i > key_units
+            if i == key_units + 1:
+                near_products()
             with region(f"wwait{i}"):
-                w_wait(i, depth - 2, depth - 1)
-            product(i, True)
+                w_wait(i, depth - 2 if late else 0, depth - 1)
+            product(i, late)
+            if i <= key_units:
+                forward(i)
+            elif i > key_units + 1:
+                forward(i - 1)
 
         @pl.when(jnp.logical_not(ends))
         def _(i=i):
+            if i == key_units:
+                w_relay(2, 3)
+                w_relay(2, 4)
             product(i, False)
-
-        if i > 0:
-            forward(i - 1)
+            if i > 0:
+                forward(i - 1)
+
         if i == 1:
             with region("early"):
                 decode_early()
@@ -866,19 +878,26 @@
             rcv[s] = snd[mine]
             rcv_stats[s] = snd_stats[mine]
             got(rcv_stats.at[: n - 1], e_recv)
+            shares = []
+            for j in range(share):
+                at = 2 * slots * j
+                peaks = rcv_stats[:, :, at : at + 1]
+                scale = jnp.exp(peaks - jnp.max(peaks, axis=0, keepdims=True))
+                total = jnp.sum(scale * rcv_stats[:, :, at + slots : at + slots + 1], axis=0)
+                shares.append((scale, total))
             got(rcv.at[: n - 1], d_recv)
             landed = rcv[...].astype(f32)
             attended = []
-            for j in range(share):
-                at = 2 * slots * j
-                peaks = rcv_stats[:, :, at : at + 1]
-                sums = rcv_stats[:, :, at + slots : at + slots + 1]
-                scale = jnp.exp(peaks - jnp.max(peaks, axis=0, keepdims=True))
+            for j, (scale, total) in enumerate(shares):
                 mixed = jnp.sum(scale * landed[:, j * pair : (j + 1) * pair], axis=0)
-                attended.append(mixed / jnp.sum(scale * sums, axis=0))
+                attended.append(mixed / total)
             att[mine] = jnp.concatenate(attended, axis=0).astype(bf16)
-            for o in range(1, n):
-                t_copy(lax.rem(s + o, n)).start()
+            for to in range(n):
+
+                @pl.when(to != s)
+                def _(to=to):
+                    t_copy(to).start()
+
             sent(snd.at[: mergers - 1], d_send)
             sent(snd_stats.at[: mergers - 1], e_send)
 
@@ -996,7 +1015,7 @@
             pltpu.VMEM((blocks, requests * nb, hd), bf16),
             pltpu.VMEM((blocks, requests * nb, hd), f32),
             pltpu.VMEM((blocks, requests * nb, hd), f32),
-            pltpu.VMEM((B, blocks, requests * nb, hd), f32),
+            pltpu.VMEM((B, blocks // 2, requests * nb, hd), f32),
             pltpu.VMEM((requests, rows, nb), bf16),
             pltpu.VMEM(out_weight.shape, bf16),
             pltpu.VMEM((requests, heads, res, hd), bf16),

time: 102 us -> 99.7 us (0.977)
  Pallas kernels: 101 us -> 98.9 us
    pallas_call x1, Pallas kernels: 99.6 us -> 97 us  [fused_body(): pl.pallas_call(functools.partial(fused_kernel, n), out_shape=(jax.ShapeDt...]
where the time goes in v5:
time: 99.7 us; the launch traced here: 99.5 us
  Pallas kernels  98.9 us (99%)
    pallas_call x1, Pallas kernels, fused_body(): pl.pallas_call(functools.partial(fused_kernel, n), out_shape=(jax.ShapeDt...  97 us

profile of v5, /device:TPU:0, one launch (start us, length us, event | category | flops | bytes accessed | tf_op | source)
XLA Modules:
  0.0 99.5 jit_solution(16150845541142727632)
XLA Ops:
  0.6 97.0 %shard_map.139 = (bf16[256,4,128]{2,1,0:T(4,128)(2,1)}, bf16[256,4,128]{2,1,0:T(4,128)(2,1)}, f32[2,8,512]{2,1,0:T(8,128)}) custom-call(s32[2]{0:T(128)} %phase_ref.1, s32[2,16]{1,0:T(2,128)} %ratio_ref.1, s32[2,16]{1,0:T(2,128)} %rlen_ref.1, bf16[2,1024,4,128]{3,2,1,0:T(4,128)(2,1)} %k_hbm.1, bf16[2,1024,4,128]{3,2,1,0:T(4,128)(2,1)} %v_hbm.1, ...), custom_call_target="tpu_custom_call" | custom-call | tf_op jit(solution)/shard_map/pallas_call | solution.py:989
  97.7 1.8 %shard_map.140 = (bf16[256,4,128]{2,1,0:T(4,128)(2,1)}, bf16[256,4,128]{2,1,0:T(4,128)(2,1)}, bf16[4,2,512]{2,1,0:T(2,128)(2,1)}) custom-call(bf16[256,4,128]{2,1,0:T(4,128)(2,1)} %get-tuple-element.9.keys_ref, bf16[256,4,128]{2,1,0:T(4,128)(2,1)} %get-tuple-element.10.values_ref, f32[2,8,512]{2,1,0:T(8,128)} %get-tuple-element.11.part_ref), custom_call_target="tpu_custom_call" | custom-call | tf_op jit(solution)/shard_map/pallas_call | solution.py:1080

commit v6 on v5

--- a/solution.py
+++ b/solution.py
@@ -687,7 +687,7 @@
             return carry
 
         with region(f"prod{i}"):
-            lax.fori_loop(0, B, step, 0)
+            lax.fori_loop(0, B, step, 0, unroll=B if late else 1)
 
     def forward(i):
         b, count = units[i]

time: 99.7 us -> 99.7 us (level)
  no operation moved by 1% of the time
where the time goes in v6:
time: 99.7 us; the launch traced here: 99.5 us
  Pallas kernels  98.9 us (99%)
    pallas_call x1, Pallas kernels, fused_body(): pl.pallas_call(functools.partial(fused_kernel, n), out_shape=(jax.ShapeDt...  97 us

profile of v6, /device:TPU:0, one launch (start us, length us, event | category | flops | bytes accessed | tf_op | source)
XLA Modules:
  0.0 99.5 jit_solution(11969626363676769174)
XLA Ops:
  0.6 97.0 %shard_map.139 = (bf16[256,4,128]{2,1,0:T(4,128)(2,1)}, bf16[256,4,128]{2,1,0:T(4,128)(2,1)}, f32[2,8,512]{2,1,0:T(8,128)}) custom-call(s32[2]{0:T(128)} %phase_ref.1, s32[2,16]{1,0:T(2,128)} %ratio_ref.1, s32[2,16]{1,0:T(2,128)} %rlen_ref.1, bf16[2,1024,4,128]{3,2,1,0:T(4,128)(2,1)} %k_hbm.1, bf16[2,1024,4,128]{3,2,1,0:T(4,128)(2,1)} %v_hbm.1, ...), custom_call_target="tpu_custom_call" | custom-call | tf_op jit(solution)/shard_map/pallas_call | solution.py:989
  97.7 1.8 %shard_map.140 = (bf16[256,4,128]{2,1,0:T(4,128)(2,1)}, bf16[256,4,128]{2,1,0:T(4,128)(2,1)}, bf16[4,2,512]{2,1,0:T(2,128)(2,1)}) custom-call(bf16[256,4,128]{2,1,0:T(4,128)(2,1)} %get-tuple-element.9.keys_ref, bf16[256,4,128]{2,1,0:T(4,128)(2,1)} %get-tuple-element.10.values_ref, f32[2,8,512]{2,1,0:T(8,128)} %get-tuple-element.11.part_ref), custom_call_target="tpu_custom_call" | custom-call | tf_op jit(solution)/shard_map/pallas_call | solution.py:1080
